TPU v7x, 256 devices: a whole 4x4x8 slice. The times are simulated.
256 devices in a mesh: dp: 8 (over x, core), expert: 32 (over z, y).
Axes of the slice: x: 4, y: 4, z: 8, core: 2. Of those that a mesh axis runs over, the one named last changes fastest.
Arguments:
- tokens: bfloat16 [4096, 2880], P(('dp', 'expert')), may hold values from -200 to 200
- norm_gain: float32 [2880], replicated, may hold values from 0.5 to 4
- router_weight: bfloat16 [2880, 32], replicated, may hold values from -0.02734375 to 0.02734375
- router_bias: float32 [32], replicated, may hold values from -1 to 1
- expert_ids: int32 [4096, 4], P(('dp', 'expert')), may hold values from 0 to 31, all different within a row; in each aligned block of 16 rows (0 to 15, 16 to 31, ...) at most 4 rows name the same one
- placement: int32 [32], replicated, may hold values from 0 to 31, each once
- gate_up: bfloat16 [32, 2, 2880, 2880], P('expert', None, None, 'dp'), may hold values from -0.109375 to 0.109375
- gate_up_bias: float32 [32, 2, 2880], P('expert', None, 'dp'), may hold values from -3 to 3
- down_proj: bfloat16 [32, 2880, 2880], P('expert', 'dp'), may hold values from -0.109375 to 0.109375
- down_bias: float32 [32, 2880], replicated, may hold values from -3 to 3
Outputs:
- mixed: bfloat16 [4096, 2880], P(('dp', 'expert'))
Inputs may be any that keep to these rules, and one draw needn't show every extreme that they name: `expert_ids`: in the rows of one device no expert is named more than 4 times; in every draw some device names some expert exactly 4 times. `placement`: every holder index appears once.
All inputs are finite; a program needn't handle non-finite values.
Results may differ from a plain program's by a relative error of at most 0.015.
Values may be sent and summed in bfloat16 or wider, within the bound.
A program may use at most 64 MiB of HBM per device.

v0:
```python
import jax
import jax.numpy as jnp
from jax import lax
from jax.sharding import PartitionSpec as P

TOPK = 4


EPS = 1e-05
LIMIT = 7.0
ALPHA = 1.702


def normalize(tokens, norm_gain):
    values = tokens.astype(jnp.float32)
    mean_square = jnp.mean(values * values, axis=-1, keepdims=True)
    return (values * lax.rsqrt(mean_square + EPS) * norm_gain).astype(jnp.bfloat16)


def routing(normed, router_weight, router_bias, expert_ids):
    logits = jnp.dot(normed, router_weight, preferred_element_type=jnp.float32) + router_bias
    expert_range = jnp.arange(logits.shape[1], dtype=jnp.int32)
    matches = expert_ids[:, :, None] == expert_range[None, None, :]
    picked = jnp.sum(jnp.where(matches, logits[:, None, :], 0.0), axis=2)
    powers = jnp.exp(picked)
    return powers / jnp.sum(powers, axis=1, keepdims=True)


def lookup(expert_ids, placement):
    expert_range = jnp.arange(placement.shape[0], dtype=jnp.int32)
    matches = expert_ids[:, :, None] == expert_range[None, None, :]
    return jnp.sum(jnp.where(matches, placement[None, None, :], 0), axis=2)


def slot_positions(columns, experts):
    flat_ids = columns.reshape(-1)
    expert_range = jnp.arange(experts, dtype=jnp.int32)
    onehot = (flat_ids[:, None] == expert_range[None, :]).astype(jnp.int32)
    before = jnp.cumsum(onehot, axis=0) - onehot
    return jnp.sum(before * onehot, axis=1).reshape(columns.shape)


def swiglu(gate_value, up_value):
    gate_value = jnp.minimum(gate_value, LIMIT)
    up_value = jnp.clip(up_value, -LIMIT, LIMIT)
    return (up_value + 1.0) * gate_value * jax.nn.sigmoid(ALPHA * gate_value)


def body(
    tokens,
    norm_gain,
    router_weight,
    router_bias,
    expert_ids,
    placement,
    gate_up,
    gate_up_bias,
    down_proj,
    down_bias,
):
    tok_dev = tokens.shape[0]
    model_width = tokens.shape[1]
    experts = placement.shape[0]
    capacity = max(2, 2 * tok_dev * TOPK // experts)
    dp_count = lax.axis_size("dp")
    expert_count = lax.axis_size("expert")
    normed = normalize(tokens, norm_gain)
    weights = routing(normed, router_weight, router_bias, expert_ids)
    columns = lookup(expert_ids, placement)
    target_row = columns * capacity + slot_positions(columns, experts)
    targets = jnp.arange(experts * capacity, dtype=jnp.int32)
    dispatch = jnp.sum(
        (target_row[:, :, None] == targets[None, None, :]).astype(jnp.int32), axis=1
    ).astype(jnp.bfloat16)
    outgoing = jnp.dot(dispatch.T, normed, preferred_element_type=jnp.float32).astype(jnp.bfloat16)
    outgoing = outgoing.reshape(experts, capacity, model_width)
    gate_weight = gate_up[0, 0]
    up_weight = gate_up[0, 1]
    gate_bias = gate_up_bias[0, 0]
    up_bias = gate_up_bias[0, 1]
    down_weight = down_proj[0]
    group_width = gate_weight.shape[1]
    grouped = lax.all_gather(outgoing, "dp", axis=0, tiled=True)
    grouped = grouped.reshape(dp_count, experts, capacity, model_width)
    row_block = lax.all_to_all(grouped, "expert", split_axis=1, concat_axis=1, tiled=True)
    flat_rows = row_block.reshape(-1, model_width)
    gate_value = jnp.dot(flat_rows, gate_weight, preferred_element_type=jnp.float32) + gate_bias
    up_value = jnp.dot(flat_rows, up_weight, preferred_element_type=jnp.float32) + up_bias
    hidden = swiglu(gate_value, up_value).astype(jnp.bfloat16)
    hidden = hidden.reshape(row_block.shape[:-1] + (group_width,))

    def down_block(row_block):
        return jnp.dot(row_block, down_weight, preferred_element_type=jnp.float32).astype(
            jnp.bfloat16
        )

    partials = lax.map(down_block, hidden.reshape(dp_count, -1, group_width))
    partials = partials.reshape(dp_count, expert_count, capacity, model_width)
    returned_parts = lax.all_to_all(partials, "expert", split_axis=1, concat_axis=1, tiled=True)
    reduced = lax.psum_scatter(returned_parts, "dp", scatter_dimension=0, tiled=True).astype(
        jnp.float32
    )
    reduced = reduced.reshape(experts, capacity, model_width) + down_bias[:, None, :]
    returned = reduced.astype(jnp.bfloat16).reshape(experts * capacity, model_width)
    picked = (
        returned[target_row.reshape(-1)].reshape(tok_dev, TOPK, model_width).astype(jnp.float32)
    )
    return jnp.sum(weights[:, :, None] * picked, axis=1).astype(jnp.bfloat16)


def solution(mesh):
    return jax.shard_map(
        body,
        mesh=mesh,
        in_specs=(
            P(("dp", "expert"), None),
            P(),
            P(),
            P(),
            P(("dp", "expert"), None),
            P(),
            P("expert", None, None, "dp"),
            P("expert", None, "dp"),
            P("expert", "dp", None),
            P(),
        ),
        out_specs=P(("dp", "expert"), None),
        check_vma=False,
    )
```

profile of v0, /device:TPU:8, one launch (start us, length us, event | category | flops | bytes accessed | tf_op | source)
XLA Modules:
  0.0 469.4 jit_solution(8633677053848857854)
XLA Ops:
  6.5 0.9 select_reduce_fusion.1
  7.5 0.1 copy.27
  7.6 0.1 eq.23
  7.7 0.1 reduce_window_sum.11
  7.8 0.2 select_reduce_fusion
  8.0 0.1 reshape.101
  8.1 0.1 copy.28
  8.3 1.0 fusion.13
  9.3 1.4 convolution_convert_fusion.1
  10.7 0.4 copy.29
  11.1 1.1 reshape.102
  12.2 45.3 %all-gather.2.cloned.1.call-done = bf16[256,4,2880]{2,1,0:T(4,128)(2,1)} async-done(((bf16[32,4,2880]{2,1,0:T(4,128)(2,1)}), bf16[256,4,2880]{2,1,0:T(4,128)(2,1)}) %all-gather.2.cloned.1.call-update) | async-done | bytes 5898256 | tf_op jit(solution)/shard_map/all_gather | solution.py:83
  57.5 7.4 %copy.30 = bf16[8,32,4,2880]{3,2,0,1:T(4,128)(2,1)} copy(bf16[8,32,4,2880]{3,2,1,0:T(4,128)(2,1)} %bitcast.37) | data formatting | bytes 11796480 | tf_op jit(solution)/shard_map/reshape | solution.py:84
  64.9 10.3 %all-to-all-start = ((bf16[8,32,4,2880]{3,2,0,1:T(4,128)(2,1)}), bf16[8,32,4,2880]{3,2,0,1:T(4,128)(2,1)}, u32[]{:S(2)}, u32[]{:S(2)}) async-start(bf16[8,32,4,2880]{3,2,0,1:T(4,128)(2,1)} %copy.30), calls=%async_computation | async-start | bytes 12058624 | tf_op jit(solution)/shard_map/all_to_all | solution.py:85
  75.2 0.2 reduce-scatter.2.cloned.1.call-start
  75.5 138.0 %all-to-all-done = bf16[8,32,4,2880]{3,2,0,1:T(4,128)(2,1)} async-done(((bf16[8,32,4,2880]{3,2,0,1:T(4,128)(2,1)}), bf16[8,32,4,2880]{3,2,0,1:T(4,128)(2,1)}, u32[]{:S(2)}, u32[]{:S(2)}) %all-to-all-start) | async-done | bytes 5898272 | tf_op jit(solution)/shard_map/all_to_all | solution.py:85
  213.5 7.4 %copy.31 = bf16[8,32,4,2880]{3,2,1,0:T(4,128)(2,1)} copy(bf16[8,32,4,2880]{3,2,0,1:T(4,128)(2,1)} %all-to-all-done) | data formatting | bytes 11796480 | tf_op jit(solution)/shard_map/all_to_all | solution.py:85
  220.9 10.3 %reshape.104 = bf16[1024,2880]{1,0:T(8,128)(2,1)} reshape(bf16[8,32,4,2880]{3,2,1,0:T(4,128)(2,1)} %copy.31) | data formatting | bytes 11796480 | tf_op jit(solution)/shard_map/reshape | solution.py:86
  231.1 6.0 %fusion.5 = f32[1024,360]{0,1:T(8,128)S(1)} fusion(bf16[1024,2880]{1,0:T(8,128)(2,1)} %reshape.104, bf16[1,2,2880,360]{2,3,1,0:T(8,128)(2,1)} %param.18), kind=kOutput, calls=%fused_computation.8 | convolution fusion | flops 2123366400 | bytes 9623552 | tf_op jit(solution)/shard_map/dot_general | solution.py:87
  237.2 5.5 %multiply_convert_fusion = bf16[1024,360]{0,1:T(8,128)(2,1)} fusion(f32[1024,360]{0,1:T(8,128)S(1)} %fusion.5, bf16[1024,2880]{1,0:T(8,128)(2,1)S(1)} %copy-done.2, bf16[1,2,2880,360]{2,3,1,0:T(8,128)(2,1)} %param.18, f32[360]{0:T(512)S(1)} %get-tuple-element.45, f32[360]{0:T(512)S(1)} %get-tuple-element.44), kind=kOutput, calls=%fused_computation.15 | convolution fusion | flops 2127790080 | bytes 10232640 | tf_op jit(solution)/shard_map/dot_general | solution.py:88
  242.6 1.5 copy.37
  244.1 15.3 %while.10 = (s32[]{:T(128)}, bf16[8,128,2880]{1,2,0:T(8,128)(2,1)}, bf16[8,128,360]{2,1,0:T(8,128)(2,1)S(1)}, bf16[360,2880]{1,0:T(8,128)(2,1)S(1)}, s32[]{:T(128)}) while((s32[]{:T(128)}, bf16[8,128,2880]{1,2,0:T(8,128)(2,1)}, bf16[8,128,360]{2,1,0:T(8,128)(2,1)S(1)}, bf16[360,2880]{1,0:T(8,128)(2,1)S(1)}, s32[]{:T(128)}) %tuple.32), condition=%wide.region_8.9_spmd, body=%wide.region_7.8_spmd.sunk | while | flops 265789440 | bytes 2956349 | solution.py:97
  244.1 1.9 fusion.31
  246.0 2.0 fusion.31
  248.0 1.9 fusion.31
  249.9 1.9 fusion.31
  251.8 1.9 fusion.31
  253.7 1.9 fusion.31
  255.6 1.9 fusion.31
  257.5 1.9 fusion.31
  259.4 8.8 %copy.33 = bf16[8,128,2880]{2,0,1:T(8,128)(2,1)} copy(bf16[8,128,2880]{1,2,0:T(8,128)(2,1)} %get-tuple-element.27) | data formatting | bytes 11796480 | tf_op jit(solution)/shard_map/while | solution.py:97
  268.2 143.1 %all_to_all.10 = bf16[8,32,4,2880]{3,0,2,1:T(8,128)(2,1)S(1)} all-to-all(bf16[8,32,4,2880]{3,0,2,1:T(8,128)(2,1)} %bitcast.36), channel_id=1, replica_groups=mesh['dp'=8,'expert'=32] {'expert'}, dimensions={1} | all-to-all | bytes 11796480 | tf_op jit(solution)/shard_map/all_to_all | solution.py:99
  411.4 4.4 copy.34
  415.8 1.0 copy-done.3
  416.7 0.3 add.100
  417.0 0.5 add.101
  417.5 0.1 copy.36
  417.6 0.1 mul.76
  417.7 0.2 convolution_add_fusion
  418.0 0.2 select_reduce_fusion.2
  418.2 0.1 copy.26
  418.3 37.3 %reduce-scatter.2.cloned.1.call-done = bf16[1,32,4,2880]{3,1,2,0:T(8,128)(2,1)} async-done(((bf16[8,32,4,2880]{3,1,2,0:T(8,128)(2,1)}), bf16[1,32,4,2880]{3,1,2,0:T(8,128)(2,1)}) %reduce-scatter.2.cloned.1.call-update) | async-done | bytes 737296 | tf_op jit(solution)/shard_map/reduce_scatter | solution.py:100
  455.6 1.5 copy.35
  457.1 1.7 reshape.109
  458.8 1.6 add_convert_fusion
  460.4 0.8 gather_fusion
  461.2 0.2 reshape.110
  461.4 1.2 multiply_reduce_fusion
  (30 shorter events, 0.3 us)
Async XLA Ops:
  6.5 411.2 %copy-start = (bf16[2880,32]{0,1:T(8,128)(2,1)S(1)}, bf16[2880,32]{0,1:T(8,128)(2,1)}, u32[]{:S(2)}) copy-start(bf16[2880,32]{0,1:T(8,128)(2,1)} %param.14) | copy-start | bytes 552964
  6.5 51.0 %all-gather.2.cloned.1.call-start = ((), (), s32[]{:S(2)}) async-start(), calls=%async_computation.3 | async-start | bytes 6782976 | tf_op jit(solution)/shard_map/all_gather | solution.py:83
  64.9 10.6 %copy-start.7 = (f32[1,2,360]{2,1,0:T(2,128)S(1)}, f32[1,2,360]{2,1,0:T(2,128)}, u32[]{:S(2)}) copy-start(f32[1,2,360]{2,1,0:T(2,128)} %param.19) | copy-start | bytes 8644
  64.9 148.6 %all-to-all-start = ((bf16[8,32,4,2880]{3,2,0,1:T(4,128)(2,1)}), bf16[8,32,4,2880]{3,2,0,1:T(4,128)(2,1)}, u32[]{:S(2)}, u32[]{:S(2)}) async-start(bf16[8,32,4,2880]{3,2,0,1:T(4,128)(2,1)} %copy.30), calls=%async_computation | async-start | bytes 12058624 | tf_op jit(solution)/shard_map/all_to_all | solution.py:85
  75.2 380.4 %reduce-scatter.2.cloned.1.call-start = ((), (), s32[]{:S(2)}) async-start(), calls=%async_computation.4 | async-start | bytes 6782976 | tf_op jit(solution)/shard_map/reduce_scatter | solution.py:100
  231.1 6.0 %copy-start.2 = (bf16[1024,2880]{1,0:T(8,128)(2,1)S(1)}, bf16[1024,2880]{1,0:T(8,128)(2,1)}, u32[]{:S(2)}) copy-start(bf16[1024,2880]{1,0:T(8,128)(2,1)} %reshape.104) | copy-start | bytes 17694724
  237.1 7.0 %copy-start.1 = (bf16[1,360,2880]{2,1,0:T(8,128)(2,1)S(1)}, bf16[1,360,2880]{2,1,0:T(8,128)(2,1)}, u32[]{:S(2)}) copy-start(bf16[1,360,2880]{2,1,0:T(8,128)(2,1)} %param.20) | copy-start | bytes 6220804
  415.7 1.0 copy-start.3
  416.7 1.0 copy-start.4
  416.7 1.0 copy-start.5
  416.7 1.0 copy-start.8
  417.0 1.0 copy-start.6
Sparse Core Ops, SparseCore 0:
  12.3 45.1 all-gather.1
  415.9 39.6 reduce-scatter.1
where the time goes:
time: 470 us; the launch traced here: 469 us
  waiting for transfers between devices  221 us (47%)
  blocking collectives  143 us (30%)
  local copies, waits for them, and re-layouts  47.7 us (10%)
  matrix products  28.3 us (6%)
  between operations  13.6 us (3%)
  starting transfers between devices  10.6 us (2%)
  other arithmetic  5.48 us (1%)
    all_to_all x1, blocking collectives, body(): lax.all_to_all(partials, 'expert', split_axis=1, concat_axis=1, tiled=True)  143 us
    all_to_all x1, waiting for transfers between devices, body(): lax.all_to_all(grouped, 'expert', split_axis=1, concat_axis=1, tiled=True)  138 us
    all_gather x1, waiting for transfers between devices, body(): grouped = lax.all_gather(outgoing, 'dp', axis=0, tiled=True)  45.3 us
    reduce_scatter x1, waiting for transfers between devices, body(): lax.psum_scatter(returned_parts, 'dp', scatter_dimension=0, tiled=True)  37.3 us
    dot_general x8, matrix products, down_block(): jnp.dot(row_block, down_weight, preferred_element_type=jnp.float32)  15.3 us
    all_to_all x1, starting transfers between devices, body(): lax.all_to_all(grouped, 'expert', split_axis=1, concat_axis=1, tiled=True)  10.3 us
    while x2, local copies, waits for them, and re-layouts, body(): partials = lax.map(down_block, hidden.reshape(dp_count, -1, group_width))  10.3 us
    reshape x1, local copies, waits for them, and re-layouts, body(): flat_rows = row_block.reshape(-1, model_width)  10.3 us
  transfers between devices with their start and end apart: 3, of which 3 were waited for; matrix products, arithmetic and copies ran while one was open for 0% of the time, Pallas kernels for 0%

commit v1 on v0

--- a/solution.py
+++ b/solution.py
@@ -80,9 +80,8 @@
     up_bias = gate_up_bias[0, 1]
     down_weight = down_proj[0]
     group_width = gate_weight.shape[1]
-    grouped = lax.all_gather(outgoing, "dp", axis=0, tiled=True)
-    grouped = grouped.reshape(dp_count, experts, capacity, model_width)
-    row_block = lax.all_to_all(grouped, "expert", split_axis=1, concat_axis=1, tiled=True)
+    row_block = lax.all_to_all(outgoing, "expert", split_axis=0, concat_axis=0, tiled=True)
+    row_block = lax.all_gather(row_block, "dp", axis=0, tiled=False)
     flat_rows = row_block.reshape(-1, model_width)
     gate_value = jnp.dot(flat_rows, gate_weight, preferred_element_type=jnp.float32) + gate_bias
     up_value = jnp.dot(flat_rows, up_weight, preferred_element_type=jnp.float32) + up_bias
@@ -96,10 +95,10 @@
 
     partials = lax.map(down_block, hidden.reshape(dp_count, -1, group_width))
     partials = partials.reshape(dp_count, expert_count, capacity, model_width)
-    returned_parts = lax.all_to_all(partials, "expert", split_axis=1, concat_axis=1, tiled=True)
-    reduced = lax.psum_scatter(returned_parts, "dp", scatter_dimension=0, tiled=True).astype(
-        jnp.float32
-    )
+    reduced_parts = lax.psum_scatter(partials, "dp", scatter_dimension=0, tiled=True)
+    reduced_parts = reduced_parts.reshape(expert_count, capacity, model_width)
+    reduced = lax.all_to_all(reduced_parts, "expert", split_axis=0, concat_axis=0, tiled=True)
+    reduced = reduced.astype(jnp.float32)
     reduced = reduced.reshape(experts, capacity, model_width) + down_bias[:, None, :]
     returned = reduced.astype(jnp.bfloat16).reshape(experts * capacity, model_width)
     picked = (

time: 470 us -> 227 us (0.48)
  waiting for transfers between devices: 221 us -> 103 us
  blocking collectives: 143 us -> 33.4 us
  local copies, waits for them, and re-layouts: 47.7 us -> 32.6 us
    all_to_all x1, waiting for transfers between devices: 138 us -> 20 us  [body(): lax.all_to_all(reduced_parts, 'expert', split_axis=0, concat_axis=0, tile...]
    all_to_all x1, blocking collectives: 143 us -> 33.4 us  [body(): lax.all_to_all(outgoing, 'expert', split_axis=0, concat_axis=0, tiled=True)]
    all_to_all x2 -> x0, local copies, waits for them, and re-layouts: 11.8 us -> none  [the longest x1 7.38 us: body(): lax.all_to_all(grouped, 'expert', split_axis=1, concat_axis=1, tiled=True)]
    reduce_scatter x1, waiting for transfers between devices: 37.3 us -> 44.2 us  [body(): lax.psum_scatter(partials, 'dp', scatter_dimension=0, tiled=True)]
    all_gather x1, waiting for transfers between devices: 45.3 us -> 39.1 us  [body(): row_block = lax.all_gather(row_block, 'dp', axis=0, tiled=False)]
where the time goes in v1:
time: 227 us; the launch traced here: 226 us
  waiting for transfers between devices  103 us (45%)
  blocking collectives  33.4 us (15%)
  local copies, waits for them, and re-layouts  32.6 us (14%)
  matrix products  28.3 us (12%)
  between operations  13.6 us (6%)
  starting transfers between devices  10.4 us (5%)
  other arithmetic  4.22 us (2%)
    reduce_scatter x1, waiting for transfers between devices, body(): lax.psum_scatter(partials, 'dp', scatter_dimension=0, tiled=True)  44.2 us
    all_gather x1, waiting for transfers between devices, body(): row_block = lax.all_gather(row_block, 'dp', axis=0, tiled=False)  39.1 us
    all_to_all x1, blocking collectives, body(): lax.all_to_all(outgoing, 'expert', split_axis=0, concat_axis=0, tiled=True)  33.4 us
    all_to_all x1, waiting for transfers between devices, body(): lax.all_to_all(reduced_parts, 'expert', split_axis=0, concat_axis=0, tile...  20 us
    dot_general x8, matrix products, down_block(): jnp.dot(row_block, down_weight, preferred_element_type=jnp.float32)  15.3 us
    all_to_all x1, starting transfers between devices, body(): lax.all_to_all(reduced_parts, 'expert', split_axis=0, concat_axis=0, tile...  10.3 us
    while x2, local copies, waits for them, and re-layouts, body(): partials = lax.map(down_block, hidden.reshape(dp_count, -1, group_width))  10.3 us
    reshape x1, local copies, waits for them, and re-layouts, body(): flat_rows = row_block.reshape(-1, model_width)  10.2 us
  transfers between devices with their start and end apart: 3, of which 3 were waited for; matrix products, arithmetic and copies ran while one was open for 0% of the time, Pallas kernels for 0%

profile of v1, /device:TPU:8, one launch (start us, length us, event | category | flops | bytes accessed | tf_op | source)
XLA Modules:
  0.0 225.8 jit_solution(2390428245021670845)
XLA Ops:
  6.5 0.9 select_reduce_fusion.1
  7.5 0.1 copy.31
  7.6 0.1 eq.23
  7.7 0.1 fusion.16
  7.7 0.1 reduce_window_sum.11
  7.8 0.2 select_reduce_fusion
  8.0 0.1 reshape.95
  8.1 0.1 copy.32
  8.2 0.1 convert_reduce_fusion
  8.3 1.0 fusion.13
  9.3 1.4 convolution_convert_fusion.1
  10.7 0.4 copy.33
  11.1 0.2 reshape.96
  11.3 33.4 %all_to_all.10 = bf16[32,4,2880]{2,1,0:T(4,128)(2,1)} all-to-all(bf16[32,4,2880]{2,1,0:T(4,128)(2,1)S(1)} %reshape.96), channel_id=1, replica_groups=mesh['dp'=8,'expert'=32] {'expert'}, dimensions={0} | all-to-all | bytes 1474560 | tf_op jit(solution)/shard_map/all_to_all | solution.py:83
  44.6 0.0 all-gather.3.cloned.1.call-update
  44.7 0.0 reduce-scatter.2.cloned.1.call-start
  44.8 39.1 %all-gather.3.cloned.1.call-done = bf16[256,4,2880]{2,1,0:T(4,128)(2,1)} async-done(((bf16[32,4,2880]{2,1,0:T(4,128)(2,1)}), bf16[256,4,2880]{2,1,0:T(4,128)(2,1)}) %all-gather.3.cloned.1.call-update) | async-done | bytes 5898256 | tf_op jit(solution)/shard_map/all_gather | solution.py:84
  83.8 10.2 %reshape.97 = bf16[1024,2880]{1,0:T(8,128)(2,1)} reshape(bf16[256,4,2880]{2,1,0:T(4,128)(2,1)} %all-gather.3.cloned.1.call-done) | data formatting | bytes 11796480 | tf_op jit(solution)/shard_map/reshape | solution.py:85
  94.1 6.0 %fusion.5 = f32[1024,360]{0,1:T(8,128)S(1)} fusion(bf16[1024,2880]{1,0:T(8,128)(2,1)} %reshape.97, bf16[1,2,2880,360]{2,3,1,0:T(8,128)(2,1)} %param.18), kind=kOutput, calls=%fused_computation.8 | convolution fusion | flops 2123366400 | bytes 9623552 | tf_op jit(solution)/shard_map/dot_general | solution.py:86
  100.1 0.0 copy-start.1
  100.1 5.5 %multiply_convert_fusion = bf16[1024,360]{0,1:T(8,128)(2,1)} fusion(f32[1024,360]{0,1:T(8,128)S(1)} %fusion.5, bf16[1024,2880]{1,0:T(8,128)(2,1)S(1)} %copy-done.2, bf16[1,2,2880,360]{2,3,1,0:T(8,128)(2,1)} %param.18, f32[360]{0:T(512)S(1)} %get-tuple-element.49, f32[360]{0:T(512)S(1)} %get-tuple-element.48), kind=kOutput, calls=%fused_computation.15 | convolution fusion | flops 2127790080 | bytes 10232640 | tf_op jit(solution)/shard_map/dot_general | solution.py:87
  105.6 1.5 copy.39
  107.0 15.3 %while.10 = (s32[]{:T(128)}, bf16[8,128,2880]{1,2,0:T(8,128)(2,1)}, bf16[8,128,360]{2,1,0:T(8,128)(2,1)S(1)}, bf16[360,2880]{1,0:T(8,128)(2,1)S(1)}, s32[]{:T(128)}) while((s32[]{:T(128)}, bf16[8,128,2880]{1,2,0:T(8,128)(2,1)}, bf16[8,128,360]{2,1,0:T(8,128)(2,1)S(1)}, bf16[360,2880]{1,0:T(8,128)(2,1)S(1)}, s32[]{:T(128)}) %tuple.33), condition=%wide.region_8.9_spmd, body=%wide.region_7.8_spmd.sunk | while | flops 265789440 | bytes 2956349 | solution.py:96
  107.1 1.9 fusion.31
  109.0 2.0 fusion.31
  110.9 1.9 fusion.31
  112.8 1.9 fusion.31
  114.7 1.9 fusion.31
  116.6 1.9 fusion.31
  118.5 1.9 fusion.31
  120.4 1.9 fusion.31
  122.3 8.8 %copy.35 = bf16[8,128,2880]{2,0,1:T(8,128)(2,1)} copy(bf16[8,128,2880]{1,2,0:T(8,128)(2,1)} %get-tuple-element.27) | data formatting | bytes 11796480 | tf_op jit(solution)/shard_map/while | solution.py:96
  131.1 7.1 %copy.36 = bf16[8,32,4,2880]{3,1,2,0:T(8,128)(2,1)} copy(bf16[8,32,4,2880]{3,0,2,1:T(8,128)(2,1)} %bitcast.36) | data formatting | bytes 11796480 | tf_op jit(solution)/shard_map/reshape | solution.py:97
  138.3 0.0 reduce-scatter.2.cloned.1.call-update
  138.3 44.2 %reduce-scatter.2.cloned.1.call-done = bf16[1,32,4,2880]{3,1,2,0:T(8,128)(2,1)} async-done(((bf16[8,32,4,2880]{3,1,2,0:T(8,128)(2,1)}), bf16[1,32,4,2880]{3,1,2,0:T(8,128)(2,1)}) %reduce-scatter.2.cloned.1.call-update) | async-done | bytes 737296 | tf_op jit(solution)/shard_map/reduce_scatter | solution.py:98
  182.6 2.4 %copy.37 = bf16[32,4,2880]{2,1,0:T(4,128)(2,1)} copy(bf16[32,4,2880]{2,0,1:T(8,128)(2,1)} %bitcast.38) | data formatting | bytes 1474560 | tf_op jit(solution)/shard_map/reshape | solution.py:99
  185.0 10.3 %all-to-all-start.1 = ((bf16[32,4,2880]{2,1,0:T(4,128)(2,1)}), bf16[32,4,2880]{2,1,0:T(4,128)(2,1)S(1)}, u32[]{:S(2)}, u32[]{:S(2)}) async-start(bf16[32,4,2880]{2,1,0:T(4,128)(2,1)} %copy.37), calls=%async_computation.2 | async-start | bytes 1507328 | tf_op jit(solution)/shard_map/all_to_all | solution.py:100
  195.3 0.1 copy.38
  195.4 0.1 mul.76
  195.5 0.2 convolution_add_fusion
  195.8 0.2 select_reduce_fusion.2
  196.0 0.1 copy.30
  196.1 20.0 %all-to-all-done.1 = bf16[32,4,2880]{2,1,0:T(4,128)(2,1)S(1)} async-done(((bf16[32,4,2880]{2,1,0:T(4,128)(2,1)}), bf16[32,4,2880]{2,1,0:T(4,128)(2,1)S(1)}, u32[]{:S(2)}, u32[]{:S(2)}) %all-to-all-start.1) | async-done | bytes 737312 | tf_op jit(solution)/shard_map/all_to_all | solution.py:100
  216.1 0.4 add_convert_fusion
  216.5 0.4 reshape.100
  216.8 0.8 gather_fusion
  217.6 0.2 reshape.101
  217.8 1.2 multiply_reduce_fusion
  (26 shorter events, 0.1 us)
Async XLA Ops:
  6.5 189.0 %copy-start = (bf16[2880,32]{0,1:T(8,128)(2,1)S(1)}, bf16[2880,32]{0,1:T(8,128)(2,1)}, u32[]{:S(2)}) copy-start(bf16[2880,32]{0,1:T(8,128)(2,1)} %param.14) | copy-start | bytes 552964
  6.5 77.3 %all-gather.3.cloned.1.call-start = ((), (), s32[]{:S(2)}) async-start(), calls=%async_computation.4 | async-start | bytes 6782976 | tf_op jit(solution)/shard_map/all_gather | solution.py:84
  11.1 33.6 %copy-start.7 = (f32[1,2,360]{2,1,0:T(2,128)S(1)}, f32[1,2,360]{2,1,0:T(2,128)}, u32[]{:S(2)}) copy-start(f32[1,2,360]{2,1,0:T(2,128)} %param.19) | copy-start | bytes 8644
  44.7 137.9 %reduce-scatter.2.cloned.1.call-start = ((), (), s32[]{:S(2)}) async-start(), calls=%async_computation.3 | async-start | bytes 6782976 | tf_op jit(solution)/shard_map/reduce_scatter | solution.py:98
  94.1 6.0 %copy-start.2 = (bf16[1024,2880]{1,0:T(8,128)(2,1)S(1)}, bf16[1024,2880]{1,0:T(8,128)(2,1)}, u32[]{:S(2)}) copy-start(bf16[1024,2880]{1,0:T(8,128)(2,1)} %reshape.97) | copy-start | bytes 17694724
  100.1 7.0 %copy-start.1 = (bf16[1,360,2880]{2,1,0:T(8,128)(2,1)S(1)}, bf16[1,360,2880]{2,1,0:T(8,128)(2,1)}, u32[]{:S(2)}) copy-start(bf16[1,360,2880]{2,1,0:T(8,128)(2,1)} %param.20) | copy-start | bytes 6220804
  138.3 57.2 %copy-start.4 = (bf16[16,2880]{1,0:T(8,128)(2,1)S(1)}, bf16[16,2880]{1,0:T(8,128)(2,1)}, u32[]{:S(2)}) copy-start(bf16[16,2880]{1,0:T(8,128)(2,1)} %param.12) | copy-start | bytes 276484
  138.3 57.2 %copy-start.5 = (f32[2880]{0:T(1024)S(1)}, f32[2880]{0:T(1024)}, u32[]{:S(2)}) copy-start(f32[2880]{0:T(1024)} %param.13) | copy-start | bytes 34564
  138.3 57.2 %copy-start.8 = (f32[32]{0:T(128)S(1)}, f32[32]{0:T(128)}, u32[]{:S(2)}) copy-start(f32[32]{0:T(128)} %param.15) | copy-start | bytes 388
  138.3 57.4 %copy-start.6 = (s32[16,4]{0,1:T(4,128)S(1)}, s32[16,4]{0,1:T(4,128)}, u32[]{:S(2)}) copy-start(s32[16,4]{0,1:T(4,128)} %param.16) | copy-start | bytes 772
  138.3 77.8 %copy-start.3 = (f32[32,2880]{1,0:T(8,128)S(1)}, f32[32,2880]{1,0:T(8,128)}, u32[]{:S(2)}) copy-start(f32[32,2880]{1,0:T(8,128)} %param.21) | copy-start | bytes 1105924
  185.0 31.1 %all-to-all-start.1 = ((bf16[32,4,2880]{2,1,0:T(4,128)(2,1)}), bf16[32,4,2880]{2,1,0:T(4,128)(2,1)S(1)}, u32[]{:S(2)}, u32[]{:S(2)}) async-start(bf16[32,4,2880]{2,1,0:T(4,128)(2,1)} %copy.37), calls=%async_computation.2 | async-start | bytes 1507328 | tf_op jit(solution)/shard_map/all_to_all | solution.py:100
Sparse Core Ops, SparseCore 0:
  44.8 39.0 all-gather.2
  138.4 44.1 reduce-scatter.1

commit v2 on v1

--- a/solution.py
+++ b/solution.py
@@ -1,7 +1,7 @@
 import jax
 import jax.numpy as jnp
 from jax import lax
-from jax.sharding import PartitionSpec as P
+from jax.sharding import Mesh, PartitionSpec as P
 
 TOPK = 4
 
@@ -62,7 +62,6 @@
     model_width = tokens.shape[1]
     experts = placement.shape[0]
     capacity = max(2, 2 * tok_dev * TOPK // experts)
-    dp_count = lax.axis_size("dp")
     expert_count = lax.axis_size("expert")
     normed = normalize(tokens, norm_gain)
     weights = routing(normed, router_weight, router_bias, expert_ids)
@@ -81,21 +80,15 @@
     down_weight = down_proj[0]
     group_width = gate_weight.shape[1]
     row_block = lax.all_to_all(outgoing, "expert", split_axis=0, concat_axis=0, tiled=True)
-    row_block = lax.all_gather(row_block, "dp", axis=0, tiled=False)
-    flat_rows = row_block.reshape(-1, model_width)
+    row_block = row_block.reshape(experts * capacity, model_width)
+    row_block = lax.all_gather(row_block, "dpx", axis=0, tiled=True)
+    flat_rows = lax.all_gather(row_block, "dpc", axis=0, tiled=True)
     gate_value = jnp.dot(flat_rows, gate_weight, preferred_element_type=jnp.float32) + gate_bias
     up_value = jnp.dot(flat_rows, up_weight, preferred_element_type=jnp.float32) + up_bias
     hidden = swiglu(gate_value, up_value).astype(jnp.bfloat16)
-    hidden = hidden.reshape(row_block.shape[:-1] + (group_width,))
-
-    def down_block(row_block):
-        return jnp.dot(row_block, down_weight, preferred_element_type=jnp.float32).astype(
-            jnp.bfloat16
-        )
-
-    partials = lax.map(down_block, hidden.reshape(dp_count, -1, group_width))
-    partials = partials.reshape(dp_count, expert_count, capacity, model_width)
-    reduced_parts = lax.psum_scatter(partials, "dp", scatter_dimension=0, tiled=True)
+    partials = jnp.dot(hidden, down_weight, preferred_element_type=jnp.float32).astype(jnp.bfloat16)
+    reduced_parts = lax.psum_scatter(partials, "dpc", scatter_dimension=0, tiled=True)
+    reduced_parts = lax.psum_scatter(reduced_parts, "dpx", scatter_dimension=0, tiled=True)
     reduced_parts = reduced_parts.reshape(expert_count, capacity, model_width)
     reduced = lax.all_to_all(reduced_parts, "expert", split_axis=0, concat_axis=0, tiled=True)
     reduced = reduced.astype(jnp.float32)
@@ -108,21 +101,28 @@
 
 
 def solution(mesh):
+    dp_size = mesh.shape["dp"]
+    cores = 2 if dp_size % 2 == 0 else 1
+    split_mesh = Mesh(
+        mesh.devices.reshape(dp_size // cores, cores, mesh.shape["expert"]),
+        ("dpx", "dpc", "expert"),
+    )
+    dp = ("dpx", "dpc")
     return jax.shard_map(
         body,
-        mesh=mesh,
+        mesh=split_mesh,
         in_specs=(
-            P(("dp", "expert"), None),
+            P(("dpx", "dpc", "expert"), None),
             P(),
             P(),
             P(),
-            P(("dp", "expert"), None),
+            P(("dpx", "dpc", "expert"), None),
             P(),
-            P("expert", None, None, "dp"),
-            P("expert", None, "dp"),
-            P("expert", "dp", None),
+            P("expert", None, None, dp),
+            P("expert", None, dp),
+            P("expert", dp, None),
             P(),
         ),
-        out_specs=P(("dp", "expert"), None),
+        out_specs=P(("dpx", "dpc", "expert"), None),
         check_vma=False,
     )

time: 227 us -> 239 us (1.053)
  waiting for transfers between devices: 103 us -> 143 us
  local copies, waits for them, and re-layouts: 32.6 us -> 13.9 us
  matrix products: 28.3 us -> 19 us
    all_gather x1 -> x2, waiting for transfers between devices: 39.1 us -> 61.4 us  [the longest x1 37.8 us: body(): row_block = lax.all_gather(row_block, 'dpx', axis=0, tiled=True)]
    reduce_scatter x1 -> x2, waiting for transfers between devices: 44.2 us -> 61.4 us  [the longest x1 41.1 us: body(): lax.psum_scatter(reduced_parts, 'dpx', scatter_dimension=0, tiled=True)]
    reshape x2 -> x1, local copies, waits for them, and re-layouts: 17.3 us -> 1.23 us  [body(): row_block = row_block.reshape(experts * capacity, model_width)]
    while x2 -> x0, local copies, waits for them, and re-layouts: 10.3 us -> none  [body(): partials = lax.map(down_block, hidden.reshape(dp_count, -1, group_width))]
    dot_general x8 -> x1, matrix products: 15.3 us -> 5.21 us  [body(): jnp.dot(hidden, down_weight, preferred_element_type=jnp.float32)]
    unnamed x18 -> x17, local copies, waits for them, and re-layouts: 0.05 us -> 4.61 us
  transfers between devices with their start and end apart: 3 -> 5, of which waited for: 3 -> 5; matrix products, arithmetic and copies ran while one was open for 0% -> 1% of each run, Pallas kernels for 0% -> 0%
where the time goes in v2:
time: 239 us; the launch traced here: 238 us
  waiting for transfers between devices  143 us (60%)
  blocking collectives  33.4 us (14%)
  matrix products  19 us (8%)
  local copies, waits for them, and re-layouts  13.9 us (6%)
  between operations  13.3 us (6%)
  starting transfers between devices  10.3 us (4%)
  other arithmetic  5.2 us (2%)
    reduce_scatter x1, waiting for transfers between devices, body(): lax.psum_scatter(reduced_parts, 'dpx', scatter_dimension=0, tiled=True)  41.1 us
    all_gather x1, waiting for transfers between devices, body(): row_block = lax.all_gather(row_block, 'dpx', axis=0, tiled=True)  37.8 us
    all_to_all x1, blocking collectives, body(): lax.all_to_all(outgoing, 'expert', split_axis=0, concat_axis=0, tiled=True)  33.4 us
    all_gather x1, waiting for transfers between devices, body(): flat_rows = lax.all_gather(row_block, 'dpc', axis=0, tiled=True)  23.6 us
    reduce_scatter x1, waiting for transfers between devices, body(): lax.psum_scatter(partials, 'dpc', scatter_dimension=0, tiled=True)  20.3 us
    all_to_all x1, waiting for transfers between devices, body(): lax.all_to_all(reduced_parts, 'expert', split_axis=0, concat_axis=0, tile...  20 us
    all_to_all x1, starting transfers between devices, body(): lax.all_to_all(reduced_parts, 'expert', split_axis=0, concat_axis=0, tile...  10.2 us
    dot_general x1, matrix products, body(): jnp.dot(flat_rows, gate_weight, preferred_element_type=jnp.float32)  5.98 us
  transfers between devices with their start and end apart: 5, of which 5 were waited for; matrix products, arithmetic and copies ran while one was open for 1% of the time, Pallas kernels for 0%

profile of v2, /device:TPU:8, one launch (start us, length us, event | category | flops | bytes accessed | tf_op | source)
XLA Modules:
  0.0 238.0 jit_solution(8380202846760216413)
XLA Ops:
  6.5 1.1 select_reduce_fusion.1
  7.6 0.1 copy.21
  7.7 0.1 eq.23
  7.8 0.1 fusion.12
  7.9 0.1 reduce_window_sum.11
  8.0 0.2 select_reduce_fusion
  8.1 0.1 reshape.92
  8.2 0.1 copy.22
  8.3 0.1 convert_reduce_fusion
  8.4 1.0 fusion.9
  9.5 2.3 convolution_convert_fusion.1
  11.7 1.5 copy.23
  13.2 1.1 reshape.93
  14.2 33.4 %all_to_all.10 = bf16[32,4,2880]{2,1,0:T(4,128)(2,1)S(1)} all-to-all(bf16[32,4,2880]{2,1,0:T(4,128)(2,1)} %reshape.93), channel_id=1, replica_groups=mesh['dpx'=4,'dpc'=2,'expert'=32] {'expert'}, dimensions={0} | all-to-all | bytes 1474560 | tf_op jit(solution)/shard_map/all_to_all | solution.py:82
  47.7 1.2 reshape.94
  48.9 0.0 all-gather.3.cloned.1.call-update
  48.9 0.0 all-gather.5.cloned.1.call-start
  49.0 37.8 %all-gather.3.cloned.1.call-done = bf16[512,2880]{1,0:T(8,128)(2,1)} async-done(((bf16[128,2880]{1,0:T(8,128)(2,1)}), bf16[512,2880]{1,0:T(8,128)(2,1)}) %all-gather.3.cloned.1.call-update) | async-done | bytes 2949136 | tf_op jit(solution)/shard_map/all_gather | solution.py:84
  86.7 0.0 all-gather.5.cloned.1.call-update
  86.8 0.0 reduce-scatter.5.cloned.1.call-start
  86.8 23.6 %all-gather.5.cloned.1.call-done = bf16[1024,2880]{1,0:T(8,128)(2,1)} async-done(((bf16[512,2880]{1,0:T(8,128)(2,1)}), bf16[1024,2880]{1,0:T(8,128)(2,1)}) %all-gather.5.cloned.1.call-update) | async-done | bytes 5898256 | tf_op jit(solution)/shard_map/all_gather | solution.py:85
  110.5 6.0 %fusion.1 = f32[1024,360]{0,1:T(8,128)S(1)} fusion(bf16[1024,2880]{1,0:T(8,128)(2,1)} %all-gather.5.cloned.1.call-done, bf16[1,2,2880,360]{2,3,1,0:T(8,128)(2,1)} %param.16), kind=kOutput, calls=%fused_computation.4 | convolution fusion | flops 2123366400 | bytes 9623552 | tf_op jit(solution)/shard_map/dot_general | solution.py:86
  116.5 4.4 %multiply_convert_fusion = bf16[1024,360]{0,1:T(8,128)(2,1)S(1)} fusion(f32[1024,360]{0,1:T(8,128)S(1)} %fusion.1, bf16[1024,2880]{1,0:T(8,128)(2,1)S(1)} %copy-done.6, bf16[1,2,2880,360]{2,3,1,0:T(8,128)(2,1)} %param.16, f32[360]{0:T(512)S(1)} %get-tuple-element.6, f32[360]{0:T(512)S(1)} %get-tuple-element.5), kind=kOutput, calls=%fused_computation.11 | convolution fusion | flops 2127790080 | bytes 10232640 | tf_op jit(solution)/shard_map/dot_general | solution.py:87
  121.0 5.2 %convolution_convert_fusion = bf16[1024,2880]{0,1:T(8,128)(2,1)} fusion(bf16[1024,360]{0,1:T(8,128)(2,1)S(1)} %multiply_convert_fusion, bf16[1,360,2880]{2,1,0:T(8,128)(2,1)S(1)} %copy-done), kind=kOutput, calls=%fused_computation.1 | convolution fusion | flops 2126315520 | bytes 8709120 | tf_op jit(solution)/shard_map/dot_general | solution.py:89
  126.2 0.0 reduce-scatter.5.cloned.1.call-update
  126.2 0.0 reduce-scatter.7.cloned.1.call-start
  126.2 20.3 %reduce-scatter.5.cloned.1.call-done = bf16[512,2880]{0,1:T(8,128)(2,1)} async-done(((bf16[1024,2880]{0,1:T(8,128)(2,1)}), bf16[512,2880]{0,1:T(8,128)(2,1)}) %reduce-scatter.5.cloned.1.call-update) | async-done | bytes 2949136 | tf_op jit(solution)/shard_map/reduce_scatter | solution.py:90
  146.5 4.6 %copy.26 = bf16[512,2880]{1,0:T(8,128)(2,1)} copy(bf16[512,2880]{0,1:T(8,128)(2,1)} %reduce-scatter.5.cloned.1.call-done) | data formatting | bytes 5898240
  151.1 0.0 reduce-scatter.7.cloned.1.call-update
  151.1 0.0 copy-start.2
  151.1 0.0 copy-start.3
  151.1 0.0 copy-start.7
  151.1 0.0 copy-start.1
  151.2 41.1 %reduce-scatter.7.cloned.1.call-done = bf16[128,2880]{1,0:T(8,128)(2,1)} async-done(((bf16[512,2880]{1,0:T(8,128)(2,1)}), bf16[128,2880]{1,0:T(8,128)(2,1)}) %reduce-scatter.7.cloned.1.call-update) | async-done | bytes 737296 | tf_op jit(solution)/shard_map/reduce_scatter | solution.py:91
  192.3 2.4 reshape.95
  194.6 10.2 %all-to-all-start.1 = ((bf16[32,4,2880]{2,1,0:T(4,128)(2,1)}), bf16[32,4,2880]{2,1,0:T(4,128)(2,1)S(1)}, u32[]{:S(2)}, u32[]{:S(2)}) async-start(bf16[32,4,2880]{2,1,0:T(4,128)(2,1)} %reshape.95), calls=%async_computation.2 | async-start | bytes 1507328 | tf_op jit(solution)/shard_map/all_to_all | solution.py:93
  204.8 0.1 copy.25
  204.9 0.1 mul.76
  205.0 1.1 convolution_add_fusion
  206.2 0.0 copy-done.4
  206.2 0.2 select_reduce_fusion.2
  206.4 0.1 copy.20
  206.5 20.0 %all-to-all-done.1 = bf16[32,4,2880]{2,1,0:T(4,128)(2,1)S(1)} async-done(((bf16[32,4,2880]{2,1,0:T(4,128)(2,1)}), bf16[32,4,2880]{2,1,0:T(4,128)(2,1)S(1)}, u32[]{:S(2)}, u32[]{:S(2)}) %all-to-all-start.1) | async-done | bytes 737312 | tf_op jit(solution)/shard_map/all_to_all | solution.py:93
  226.5 1.3 add_convert_fusion
  227.7 1.6 reshape.96
  229.3 0.8 gather_fusion
  230.1 0.2 reshape.97
  230.3 1.2 multiply_reduce_fusion
  (19 shorter events, 0.1 us)
Async XLA Ops:
  6.5 114.4 %copy-start = (bf16[1,360,2880]{2,1,0:T(8,128)(2,1)S(1)}, bf16[1,360,2880]{2,1,0:T(8,128)(2,1)}, u32[]{:S(2)}) copy-start(bf16[1,360,2880]{2,1,0:T(8,128)(2,1)} %param.18) | copy-start | bytes 6220804
  6.5 80.2 %all-gather.3.cloned.1.call-start = ((), (), s32[]{:S(2)}) async-start(), calls=%async_computation.4 | async-start | bytes 3768320 | tf_op jit(solution)/shard_map/all_gather | solution.py:84
  48.9 37.9 %copy-start.5 = (f32[1,2,360]{2,1,0:T(2,128)S(1)}, f32[1,2,360]{2,1,0:T(2,128)}, u32[]{:S(2)}) copy-start(f32[1,2,360]{2,1,0:T(2,128)} %param.17) | copy-start | bytes 8644
  48.9 61.6 %all-gather.5.cloned.1.call-start = ((), (), s32[]{:S(2)}) async-start(), calls=%async_computation.5 | async-start | bytes 9043968 | tf_op jit(solution)/shard_map/all_gather | solution.py:85
  86.8 59.7 %reduce-scatter.5.cloned.1.call-start = ((), (), s32[]{:S(2)}) async-start(), calls=%async_computation.6 | async-start | bytes 8847360 | tf_op jit(solution)/shard_map/reduce_scatter | solution.py:90
  110.5 6.0 %copy-start.6 = (bf16[1024,2880]{1,0:T(8,128)(2,1)S(1)}, bf16[1024,2880]{1,0:T(8,128)(2,1)}, u32[]{:S(2)}) copy-start(bf16[1024,2880]{1,0:T(8,128)(2,1)} %all-gather.5.cloned.1.call-done) | copy-start | bytes 17694724
  126.2 66.1 %reduce-scatter.7.cloned.1.call-start = ((), (), s32[]{:S(2)}) async-start(), calls=%async_computation.7 | async-start | bytes 3768320 | tf_op jit(solution)/shard_map/reduce_scatter | solution.py:91
  151.1 53.9 %copy-start.2 = (bf16[16,2880]{1,0:T(8,128)(2,1)S(1)}, bf16[16,2880]{1,0:T(8,128)(2,1)}, u32[]{:S(2)}) copy-start(bf16[16,2880]{1,0:T(8,128)(2,1)} %param.10) | copy-start | bytes 276484
  151.1 53.9 %copy-start.3 = (f32[2880]{0:T(1024)S(1)}, f32[2880]{0:T(1024)}, u32[]{:S(2)}) copy-start(f32[2880]{0:T(1024)} %param.11) | copy-start | bytes 34564
  151.1 53.9 %copy-start.7 = (f32[32]{0:T(128)S(1)}, f32[32]{0:T(128)}, u32[]{:S(2)}) copy-start(f32[32]{0:T(128)} %param.13) | copy-start | bytes 388
  151.1 55.0 %copy-start.4 = (s32[16,4]{0,1:T(4,128)S(1)}, s32[16,4]{0,1:T(4,128)}, u32[]{:S(2)}) copy-start(s32[16,4]{0,1:T(4,128)} %param.14) | copy-start | bytes 772
  151.1 75.3 %copy-start.1 = (f32[32,2880]{1,0:T(8,128)S(1)}, f32[32,2880]{1,0:T(8,128)}, u32[]{:S(2)}) copy-start(f32[32,2880]{1,0:T(8,128)} %param.19) | copy-start | bytes 1105924
  194.6 31.8 %all-to-all-start.1 = ((bf16[32,4,2880]{2,1,0:T(4,128)(2,1)}), bf16[32,4,2880]{2,1,0:T(4,128)(2,1)S(1)}, u32[]{:S(2)}, u32[]{:S(2)}) async-start(bf16[32,4,2880]{2,1,0:T(4,128)(2,1)} %reshape.95), calls=%async_computation.2 | async-start | bytes 1507328 | tf_op jit(solution)/shard_map/all_to_all | solution.py:93
Sparse Core Ops, SparseCore 0:
  49.0 37.6 all-gather.2
  88.5 21.9 all-gather.4
  126.3 20.1 reduce-scatter.4
  151.2 41.0 reduce-scatter.6

commit v3 on v1

--- a/solution.py
+++ b/solution.py
@@ -62,7 +62,6 @@
     model_width = tokens.shape[1]
     experts = placement.shape[0]
     capacity = max(2, 2 * tok_dev * TOPK // experts)
-    dp_count = lax.axis_size("dp")
     expert_count = lax.axis_size("expert")
     normed = normalize(tokens, norm_gain)
     weights = routing(normed, router_weight, router_bias, expert_ids)
@@ -81,20 +80,12 @@
     down_weight = down_proj[0]
     group_width = gate_weight.shape[1]
     row_block = lax.all_to_all(outgoing, "expert", split_axis=0, concat_axis=0, tiled=True)
-    row_block = lax.all_gather(row_block, "dp", axis=0, tiled=False)
-    flat_rows = row_block.reshape(-1, model_width)
+    row_block = row_block.reshape(experts * capacity, model_width)
+    flat_rows = lax.all_gather(row_block, "dp", axis=0, tiled=True)
     gate_value = jnp.dot(flat_rows, gate_weight, preferred_element_type=jnp.float32) + gate_bias
     up_value = jnp.dot(flat_rows, up_weight, preferred_element_type=jnp.float32) + up_bias
     hidden = swiglu(gate_value, up_value).astype(jnp.bfloat16)
-    hidden = hidden.reshape(row_block.shape[:-1] + (group_width,))
-
-    def down_block(row_block):
-        return jnp.dot(row_block, down_weight, preferred_element_type=jnp.float32).astype(
-            jnp.bfloat16
-        )
-
-    partials = lax.map(down_block, hidden.reshape(dp_count, -1, group_width))
-    partials = partials.reshape(dp_count, expert_count, capacity, model_width)
+    partials = jnp.dot(hidden, down_weight, preferred_element_type=jnp.float32).astype(jnp.bfloat16)
     reduced_parts = lax.psum_scatter(partials, "dp", scatter_dimension=0, tiled=True)
     reduced_parts = reduced_parts.reshape(expert_count, capacity, model_width)
     reduced = lax.all_to_all(reduced_parts, "expert", split_axis=0, concat_axis=0, tiled=True)

time: 227 us -> 203 us (0.89)
  local copies, waits for them, and re-layouts: 32.6 us -> 17.8 us
  matrix products: 28.3 us -> 19 us
    reshape x2 -> x1, local copies, waits for them, and re-layouts: 17.3 us -> 1.24 us  [body(): row_block = row_block.reshape(experts * capacity, model_width)]
    while x2 -> x0, local copies, waits for them, and re-layouts: 10.3 us -> none  [body(): partials = lax.map(down_block, hidden.reshape(dp_count, -1, group_width))]
    dot_general x8 -> x1, matrix products: 15.3 us -> 5.2 us  [body(): jnp.dot(hidden, down_weight, preferred_element_type=jnp.float32)]
    unnamed x18 -> x17, local copies, waits for them, and re-layouts: 0.05 us -> 8.55 us
  transfers between devices with their start and end apart: 3 -> 3, of which waited for: 3 -> 3; matrix products, arithmetic and copies ran while one was open for 0% -> 1% of each run, Pallas kernels for 0% -> 0%
where the time goes in v3:
time: 203 us; the launch traced here: 202 us
  waiting for transfers between devices  103 us (51%)
  blocking collectives  33.4 us (16%)
  matrix products  19 us (9%)
  local copies, waits for them, and re-layouts  17.8 us (9%)
  between operations  13.6 us (7%)
  starting transfers between devices  10.2 us (5%)
  other arithmetic  5.2 us (3%)
    reduce_scatter x1, waiting for transfers between devices, body(): lax.psum_scatter(partials, 'dp', scatter_dimension=0, tiled=True)  44.2 us
    all_gather x1, waiting for transfers between devices, body(): flat_rows = lax.all_gather(row_block, 'dp', axis=0, tiled=True)  39.1 us
    all_to_all x1, blocking collectives, body(): lax.all_to_all(outgoing, 'expert', split_axis=0, concat_axis=0, tiled=True)  33.4 us
    all_to_all x1, waiting for transfers between devices, body(): lax.all_to_all(reduced_parts, 'expert', split_axis=0, concat_axis=0, tile...  19.3 us
    all_to_all x1, starting transfers between devices, body(): lax.all_to_all(reduced_parts, 'expert', split_axis=0, concat_axis=0, tile...  10.2 us
    unnamed x17, local copies, waits for them, and re-layouts  8.55 us
    dot_general x1, matrix products, body(): jnp.dot(flat_rows, gate_weight, preferred_element_type=jnp.float32)  5.98 us
    dot_general x1, matrix products, body(): jnp.dot(hidden, down_weight, preferred_element_type=jnp.float32)  5.2 us
  transfers between devices with their start and end apart: 3, of which 3 were waited for; matrix products, arithmetic and copies ran while one was open for 1% of the time, Pallas kernels for 0%

profile of v3, /device:TPU:8, one launch (start us, length us, event | category | flops | bytes accessed | tf_op | source)
XLA Modules:
  0.0 201.9 jit_solution(5373653230099547077)
XLA Ops:
  6.5 0.0 copy-start
  6.5 0.0 all-gather.2.cloned.1.call-start
  6.5 1.1 select_reduce_fusion.1
  7.6 0.1 copy.21
  7.7 0.1 eq.23
  7.8 0.1 fusion.12
  7.9 0.1 reduce_window_sum.11
  8.0 0.2 select_reduce_fusion
  8.1 0.1 reshape.92
  8.2 0.1 copy.22
  8.3 0.1 convert_reduce_fusion
  8.4 1.0 fusion.9
  9.5 2.3 %convolution_convert_fusion.1 = bf16[128,2880]{0,1:T(8,128)(2,1)} fusion(bf16[16,2880]{1,0:T(8,128)(2,1)} %param.10, f32[2880]{0:T(1024)} %param.11, f32[16]{0:T(128)S(1)} %add_rsqrt_fusion, s32[16,128]{1,0:T(8,128)S(1)} %convert_reduce_fusion), kind=kOutput, calls=%fused_computation.2 | convolution fusion | flops 12351488 | bytes 849216 | tf_op jit(solution)/shard_map/dot_general | solution.py:74
  11.7 1.5 copy.23
  13.2 1.1 reshape.93
  14.2 33.4 %all_to_all.10 = bf16[32,4,2880]{2,1,0:T(4,128)(2,1)S(1)} all-to-all(bf16[32,4,2880]{2,1,0:T(4,128)(2,1)} %reshape.93), channel_id=1, replica_groups=mesh['dp'=8,'expert'=32] {'expert'}, dimensions={0} | all-to-all | bytes 1474560 | tf_op jit(solution)/shard_map/all_to_all | solution.py:82
  47.7 1.2 reshape.94
  48.9 0.0 all-gather.2.cloned.1.call-update
  48.9 0.0 reduce-scatter.4.cloned.1.call-start
  49.0 0.0 copy-done.5
  49.0 39.1 %all-gather.2.cloned.1.call-done = bf16[1024,2880]{1,0:T(8,128)(2,1)} async-done(((bf16[128,2880]{1,0:T(8,128)(2,1)}), bf16[1024,2880]{1,0:T(8,128)(2,1)}) %all-gather.2.cloned.1.call-update) | async-done | bytes 5898256 | tf_op jit(solution)/shard_map/all_gather | solution.py:84
  88.1 6.0 %fusion.1 = f32[1024,360]{0,1:T(8,128)S(1)} fusion(bf16[1024,2880]{1,0:T(8,128)(2,1)} %all-gather.2.cloned.1.call-done, bf16[1,2,2880,360]{2,3,1,0:T(8,128)(2,1)} %param.16), kind=kOutput, calls=%fused_computation.4 | convolution fusion | flops 2123366400 | bytes 9623552 | tf_op jit(solution)/shard_map/dot_general | solution.py:85
  94.1 0.0 copy-done.6
  94.1 4.4 %multiply_convert_fusion = bf16[1024,360]{0,1:T(8,128)(2,1)S(1)} fusion(f32[1024,360]{0,1:T(8,128)S(1)} %fusion.1, bf16[1024,2880]{1,0:T(8,128)(2,1)S(1)} %copy-done.6, bf16[1,2,2880,360]{2,3,1,0:T(8,128)(2,1)} %param.16, f32[360]{0:T(512)S(1)} %get-tuple-element.6, f32[360]{0:T(512)S(1)} %get-tuple-element.5), kind=kOutput, calls=%fused_computation.11 | convolution fusion | flops 2127790080 | bytes 10232640 | tf_op jit(solution)/shard_map/dot_general | solution.py:86
  98.6 5.2 %convolution_convert_fusion = bf16[1024,2880]{0,1:T(8,128)(2,1)} fusion(bf16[1024,360]{0,1:T(8,128)(2,1)S(1)} %multiply_convert_fusion, bf16[1,360,2880]{2,1,0:T(8,128)(2,1)S(1)} %copy-done), kind=kOutput, calls=%fused_computation.1 | convolution fusion | flops 2126315520 | bytes 8709120 | tf_op jit(solution)/shard_map/dot_general | solution.py:88
  103.8 8.5 %copy.26 = bf16[1024,2880]{1,0:T(8,128)(2,1)} copy(bf16[1024,2880]{0,1:T(8,128)(2,1)} %convolution_convert_fusion) | data formatting | bytes 11796480
  112.3 0.0 reduce-scatter.4.cloned.1.call-update
  112.3 0.0 copy-start.2
  112.3 0.0 copy-start.3
  112.3 0.0 copy-start.7
  112.3 0.0 copy-start.4
  112.3 0.0 copy-start.1
  112.4 44.2 %reduce-scatter.4.cloned.1.call-done = bf16[128,2880]{1,0:T(8,128)(2,1)} async-done(((bf16[1024,2880]{1,0:T(8,128)(2,1)}), bf16[128,2880]{1,0:T(8,128)(2,1)}) %reduce-scatter.4.cloned.1.call-update) | async-done | bytes 737296 | tf_op jit(solution)/shard_map/reduce_scatter | solution.py:89
  156.6 2.4 %reshape.95 = bf16[32,4,2880]{2,1,0:T(4,128)(2,1)} reshape(bf16[128,2880]{1,0:T(8,128)(2,1)} %reduce-scatter.4.cloned.1.call-done) | data formatting | bytes 1474560 | tf_op jit(solution)/shard_map/reshape | solution.py:90
  159.0 10.2 %all-to-all-start.1 = ((bf16[32,4,2880]{2,1,0:T(4,128)(2,1)}), bf16[32,4,2880]{2,1,0:T(4,128)(2,1)S(1)}, u32[]{:S(2)}, u32[]{:S(2)}) async-start(bf16[32,4,2880]{2,1,0:T(4,128)(2,1)} %reshape.95), calls=%async_computation.1 | async-start | bytes 1507328 | tf_op jit(solution)/shard_map/all_to_all | solution.py:91
  169.1 0.1 copy.25
  169.2 0.1 mul.76
  169.3 1.1 convolution_add_fusion
  170.5 0.0 copy-done.4
  170.5 0.2 select_reduce_fusion.2
  170.7 0.1 copy.20
  170.8 19.3 %all-to-all-done.1 = bf16[32,4,2880]{2,1,0:T(4,128)(2,1)S(1)} async-done(((bf16[32,4,2880]{2,1,0:T(4,128)(2,1)}), bf16[32,4,2880]{2,1,0:T(4,128)(2,1)S(1)}, u32[]{:S(2)}, u32[]{:S(2)}) %all-to-all-start.1) | async-done | bytes 737312 | tf_op jit(solution)/shard_map/all_to_all | solution.py:91
  190.1 0.0 copy-done.1
  190.1 1.3 add_convert_fusion
  191.3 1.6 reshape.96
  192.9 0.8 gather_fusion
  193.7 0.2 reshape.97
  193.9 1.2 multiply_reduce_fusion
  (13 shorter events, 0.1 us)
Async XLA Ops:
  6.5 92.0 %copy-start = (bf16[1,360,2880]{2,1,0:T(8,128)(2,1)S(1)}, bf16[1,360,2880]{2,1,0:T(8,128)(2,1)}, u32[]{:S(2)}) copy-start(bf16[1,360,2880]{2,1,0:T(8,128)(2,1)} %param.18) | copy-start | bytes 6220804
  6.5 81.6 %all-gather.2.cloned.1.call-start = ((), (), s32[]{:S(2)}) async-start(), calls=%async_computation.3 | async-start | bytes 6782976 | tf_op jit(solution)/shard_map/all_gather | solution.py:84
  47.7 1.3 copy-start.5
  48.9 107.7 %reduce-scatter.4.cloned.1.call-start = ((), (), s32[]{:S(2)}) async-start(), calls=%async_computation.4 | async-start | bytes 6782976 | tf_op jit(solution)/shard_map/reduce_scatter | solution.py:89
  88.1 6.0 %copy-start.6 = (bf16[1024,2880]{1,0:T(8,128)(2,1)S(1)}, bf16[1024,2880]{1,0:T(8,128)(2,1)}, u32[]{:S(2)}) copy-start(bf16[1024,2880]{1,0:T(8,128)(2,1)} %all-gather.2.cloned.1.call-done) | copy-start | bytes 17694724
  112.3 57.0 %copy-start.2 = (bf16[16,2880]{1,0:T(8,128)(2,1)S(1)}, bf16[16,2880]{1,0:T(8,128)(2,1)}, u32[]{:S(2)}) copy-start(bf16[16,2880]{1,0:T(8,128)(2,1)} %param.10) | copy-start | bytes 276484
  112.3 57.0 %copy-start.3 = (f32[2880]{0:T(1024)S(1)}, f32[2880]{0:T(1024)}, u32[]{:S(2)}) copy-start(f32[2880]{0:T(1024)} %param.11) | copy-start | bytes 34564
  112.3 57.0 %copy-start.7 = (f32[32]{0:T(128)S(1)}, f32[32]{0:T(128)}, u32[]{:S(2)}) copy-start(f32[32]{0:T(128)} %param.13) | copy-start | bytes 388
  112.3 58.2 %copy-start.4 = (s32[16,4]{0,1:T(4,128)S(1)}, s32[16,4]{0,1:T(4,128)}, u32[]{:S(2)}) copy-start(s32[16,4]{0,1:T(4,128)} %param.14) | copy-start | bytes 772
  112.3 77.7 %copy-start.1 = (f32[32,2880]{1,0:T(8,128)S(1)}, f32[32,2880]{1,0:T(8,128)}, u32[]{:S(2)}) copy-start(f32[32,2880]{1,0:T(8,128)} %param.19) | copy-start | bytes 1105924
  159.0 31.1 %all-to-all-start.1 = ((bf16[32,4,2880]{2,1,0:T(4,128)(2,1)}), bf16[32,4,2880]{2,1,0:T(4,128)(2,1)S(1)}, u32[]{:S(2)}, u32[]{:S(2)}) async-start(bf16[32,4,2880]{2,1,0:T(4,128)(2,1)} %reshape.95), calls=%async_computation.1 | async-start | bytes 1507328 | tf_op jit(solution)/shard_map/all_to_all | solution.py:91
Sparse Core Ops, SparseCore 0:
  49.1 39.0 all-gather.1
  112.4 44.1 reduce-scatter.3

commit v4 on v3

--- a/solution.py
+++ b/solution.py
@@ -79,16 +79,26 @@
     up_bias = gate_up_bias[0, 1]
     down_weight = down_proj[0]
     group_width = gate_weight.shape[1]
-    row_block = lax.all_to_all(outgoing, "expert", split_axis=0, concat_axis=0, tiled=True)
-    row_block = row_block.reshape(experts * capacity, model_width)
-    flat_rows = lax.all_gather(row_block, "dp", axis=0, tiled=True)
-    gate_value = jnp.dot(flat_rows, gate_weight, preferred_element_type=jnp.float32) + gate_bias
-    up_value = jnp.dot(flat_rows, up_weight, preferred_element_type=jnp.float32) + up_bias
-    hidden = swiglu(gate_value, up_value).astype(jnp.bfloat16)
-    partials = jnp.dot(hidden, down_weight, preferred_element_type=jnp.float32).astype(jnp.bfloat16)
-    reduced_parts = lax.psum_scatter(partials, "dp", scatter_dimension=0, tiled=True)
-    reduced_parts = reduced_parts.reshape(expert_count, capacity, model_width)
-    reduced = lax.all_to_all(reduced_parts, "expert", split_axis=0, concat_axis=0, tiled=True)
+    chunks = 2 if capacity % 2 == 0 else 1
+    width = capacity // chunks
+
+    def expert_chunk(sent):
+        row_block = lax.all_to_all(sent, "expert", split_axis=0, concat_axis=0, tiled=True)
+        row_block = row_block.reshape(experts * width, model_width)
+        flat_rows = lax.all_gather(row_block, "dp", axis=0, tiled=True)
+        gate_value = jnp.dot(flat_rows, gate_weight, preferred_element_type=jnp.float32) + gate_bias
+        up_value = jnp.dot(flat_rows, up_weight, preferred_element_type=jnp.float32) + up_bias
+        hidden = swiglu(gate_value, up_value).astype(jnp.bfloat16)
+        partials = jnp.dot(hidden, down_weight, preferred_element_type=jnp.float32).astype(
+            jnp.bfloat16
+        )
+        reduced_parts = lax.psum_scatter(partials, "dp", scatter_dimension=0, tiled=True)
+        reduced_parts = reduced_parts.reshape(expert_count, width, model_width)
+        return lax.all_to_all(reduced_parts, "expert", split_axis=0, concat_axis=0, tiled=True)
+
+    reduced = jnp.concatenate(
+        [expert_chunk(outgoing[:, c * width : (c + 1) * width]) for c in range(chunks)], axis=1
+    )
     reduced = reduced.astype(jnp.float32)
     reduced = reduced.reshape(experts, capacity, model_width) + down_bias[:, None, :]
     returned = reduced.astype(jnp.bfloat16).reshape(experts * capacity, model_width)

time: 203 us -> 216 us (1.064)
  blocking collectives: 33.4 us -> 43.5 us
  starting transfers between devices: 10.2 us -> 20.3 us
  waiting for transfers between devices: 103 us -> 95.1 us
  local copies, waits for them, and re-layouts: 17.8 us -> 12.4 us
  matrix products: 19 us -> 24.2 us
    reduce_scatter x1 -> x2, waiting for transfers between devices: 44.2 us -> 57.1 us  [expert_chunk(): lax.psum_scatter(partials, 'dp', scatter_dimension=0, tiled=True)]
    all_gather x1 -> x2, waiting for transfers between devices: 39.1 us -> 27.4 us  [expert_chunk(): flat_rows = lax.all_gather(row_block, 'dp', axis=0, tiled=True)]
    all_to_all x1 -> x2, blocking collectives: 33.4 us -> 43.5 us  [expert_chunk(): lax.all_to_all(sent, 'expert', split_axis=0, concat_axis=0, tiled=True)]
    all_to_all x1 -> x2, starting transfers between devices: 10.2 us -> 20.1 us  [expert_chunk(): lax.all_to_all(reduced_parts, 'expert', split_axis=0, concat_axis=0, tile...]
    all_to_all x1 -> x2, waiting for transfers between devices: 19.3 us -> 10.6 us  [expert_chunk(): lax.all_to_all(reduced_parts, 'expert', split_axis=0, concat_axis=0, tile...]
    unnamed x17 -> x16, local copies, waits for them, and re-layouts: 8.55 us -> 0.04 us
    dot_general x3 -> x4, matrix products: 15.6 us -> 22.5 us  [the longest x2 14.8 us: expert_chunk(): jnp.dot(hidden, down_weight, preferred_element_type=jnp.float32)]
    reshape x3 -> x4, local copies, waits for them, and re-layouts: 5.15 us -> 5.84 us  [the longest x2 3.74 us: expert_chunk(): reduced_parts = reduced_parts.reshape(expert_count, width, model_width)]
  transfers between devices with their start and end apart: 3 -> 6, of which waited for: 3 -> 5; matrix products, arithmetic and copies ran while one was open for 1% -> 13% of each run, Pallas kernels for 0% -> 0%
where the time goes in v4:
time: 216 us; the launch traced here: 214 us
  waiting for transfers between devices  95.1 us (44%)
  blocking collectives  43.5 us (20%)
  matrix products  24.2 us (11%)
  starting transfers between devices  20.3 us (9%)
  between operations  13.3 us (6%)
  local copies, waits for them, and re-layouts  12.4 us (6%)
  other arithmetic  5.69 us (3%)
    reduce_scatter x2, waiting for transfers between devices, expert_chunk(): lax.psum_scatter(partials, 'dp', scatter_dimension=0, tiled=True)  57.1 us
    all_to_all x2, blocking collectives, expert_chunk(): lax.all_to_all(sent, 'expert', split_axis=0, concat_axis=0, tiled=True)  43.5 us
    all_gather x2, waiting for transfers between devices, expert_chunk(): flat_rows = lax.all_gather(row_block, 'dp', axis=0, tiled=True)  27.4 us
    all_to_all x2, starting transfers between devices, expert_chunk(): lax.all_to_all(reduced_parts, 'expert', split_axis=0, concat_axis=0, tile...  20.1 us
    dot_general x2, matrix products, expert_chunk(): jnp.dot(hidden, down_weight, preferred_element_type=jnp.float32)  14.8 us
    all_to_all x2, waiting for transfers between devices, expert_chunk(): lax.all_to_all(reduced_parts, 'expert', split_axis=0, concat_axis=0, tile...  10.6 us
    dot_general x2, matrix products, expert_chunk(): jnp.dot(flat_rows, gate_weight, preferred_element_type=jnp.float32)  7.71 us
  transfers between devices with their start and end apart: 6, of which 5 were waited for; matrix products, arithmetic and copies ran while one was open for 13% of the time, Pallas kernels for 0%

profile of v4, /device:TPU:8, one launch (start us, length us, event | category | flops | bytes accessed | tf_op | source)
XLA Modules:
  0.0 214.4 jit_solution(4000573040105774814)
XLA Ops:
  6.5 1.1 select_reduce_fusion.1
  7.6 0.1 copy.15
  7.7 0.1 eq.23
  7.8 0.1 fusion.89
  7.9 0.1 reduce_window_sum.11
  8.0 0.2 select_reduce_fusion
  8.1 0.1 reshape.101
  8.2 0.1 copy.16
  8.3 0.1 convert_reduce_fusion
  8.4 1.0 fusion.86
  9.5 1.4 convolution_convert_fusion.2
  10.8 1.2 copy.17
  12.0 1.7 reshape.102
  13.7 0.5 fusion.103
  14.2 25.2 %all_to_all.20 = bf16[32,2,2880]{2,1,0:T(2,128)(2,1)S(1)} all-to-all(bf16[32,2,2880]{2,1,0:T(2,128)(2,1)S(1)} %get-tuple-element.7), channel_id=1, replica_groups=mesh['dp'=8,'expert'=32] {'expert'}, dimensions={0} | all-to-all | bytes 737280 | tf_op jit(solution)/shard_map/all_to_all | solution.py:86
  39.4 1.1 reshape.103
  40.5 0.0 all-gather.3.cloned.1.call-update
  40.5 0.0 all-gather.5.cloned.1.call-start
  40.6 18.3 %all_to_all.21 = bf16[32,2,2880]{2,1,0:T(2,128)(2,1)S(1)} all-to-all(bf16[32,2,2880]{2,1,0:T(2,128)(2,1)S(1)} %get-tuple-element.8), channel_id=1, replica_groups=mesh['dp'=8,'expert'=32] {'expert'}, dimensions={0} | all-to-all | bytes 737280 | tf_op jit(solution)/shard_map/all_to_all | solution.py:86
  58.9 1.0 reshape.105
  59.9 0.0 all-gather.5.cloned.1.call-update
  59.9 0.0 reduce-scatter.3.cloned.1.call-start
  60.0 7.1 %all-gather.3.cloned.1.call-done = bf16[512,2880]{1,0:T(8,128)(2,1)} async-done(((bf16[64,2880]{1,0:T(8,128)(2,1)}), bf16[512,2880]{1,0:T(8,128)(2,1)}) %all-gather.3.cloned.1.call-update) | async-done | bytes 2949136 | tf_op jit(solution)/shard_map/all_gather | solution.py:88
  67.1 3.9 %fusion.47 = f32[512,360]{0,1:T(8,128)S(1)} fusion(bf16[512,2880]{1,0:T(8,128)(2,1)} %all-gather.3.cloned.1.call-done, bf16[1,2,2880,360]{2,3,1,0:T(8,128)(2,1)} %param.16, f32[360]{0:T(512)S(1)} %get-tuple-element.6), kind=kOutput, calls=%fused_computation.30 | convolution fusion | flops 1062051840 | bytes 5873056 | tf_op jit(solution)/shard_map/dot_general | solution.py:89
  71.0 7.4 %convolution_convert_fusion.1 = bf16[512,2880]{1,0:T(8,128)(2,1)} fusion(bf16[1,360,2880]{2,1,0:T(8,128)(2,1)S(1)} %copy-done, f32[512,360]{0,1:T(8,128)S(1)} %fusion.47, bf16[512,2880]{1,0:T(8,128)(2,1)} %all-gather.3.cloned.1.call-done, bf16[1,2,2880,360]{2,3,1,0:T(8,128)(2,1)} %param.16, f32[360]{0:T(512)S(1)} %get-tuple-element.5), kind=kOutput, calls=%fused_computation.2 | convolution fusion | flops 2126684160 | bytes 10895776 | tf_op jit(solution)/shard_map/dot_general | solution.py:92
  78.4 0.0 reduce-scatter.3.cloned.1.call-update
  78.4 0.0 reduce-scatter.5.cloned.1.call-start
  78.4 20.3 %all-gather.5.cloned.1.call-done = bf16[512,2880]{1,0:T(8,128)(2,1)} async-done(((bf16[64,2880]{1,0:T(8,128)(2,1)}), bf16[512,2880]{1,0:T(8,128)(2,1)}) %all-gather.5.cloned.1.call-update) | async-done | bytes 2949136 | tf_op jit(solution)/shard_map/all_gather | solution.py:88
  98.8 3.9 %fusion.53 = f32[512,360]{0,1:T(8,128)S(1)} fusion(bf16[512,2880]{1,0:T(8,128)(2,1)} %all-gather.5.cloned.1.call-done, bf16[1,2,2880,360]{2,3,1,0:T(8,128)(2,1)} %param.16, f32[360]{0:T(512)S(1)} %get-tuple-element.6), kind=kOutput, calls=%fused_computation.32 | convolution fusion | flops 1062051840 | bytes 5873056 | tf_op jit(solution)/shard_map/dot_general | solution.py:89
  102.6 7.4 %convolution_convert_fusion = bf16[512,2880]{1,0:T(8,128)(2,1)} fusion(bf16[1,360,2880]{2,1,0:T(8,128)(2,1)S(1)} %copy-done, f32[512,360]{0,1:T(8,128)S(1)} %fusion.53, bf16[512,2880]{1,0:T(8,128)(2,1)} %all-gather.5.cloned.1.call-done, bf16[1,2,2880,360]{2,3,1,0:T(8,128)(2,1)} %param.16, f32[360]{0:T(512)S(1)} %get-tuple-element.5), kind=kOutput, calls=%fused_computation.1 | convolution fusion | flops 2126684160 | bytes 10895776 | tf_op jit(solution)/shard_map/dot_general | solution.py:92
  110.1 0.0 reduce-scatter.5.cloned.1.call-update
  110.1 29.6 %reduce-scatter.3.cloned.1.call-done = bf16[64,2880]{1,0:T(8,128)(2,1)} async-done(((bf16[512,2880]{1,0:T(8,128)(2,1)}), bf16[64,2880]{1,0:T(8,128)(2,1)}) %reduce-scatter.3.cloned.1.call-update) | async-done | bytes 368656 | tf_op jit(solution)/shard_map/reduce_scatter | solution.py:95
  139.7 1.9 reshape.104
  141.6 10.2 %all-to-all-start.1 = ((bf16[32,2,2880]{2,1,0:T(2,128)(2,1)}), bf16[32,2,2880]{2,1,0:T(2,128)(2,1)S(1)}, u32[]{:S(2)}, u32[]{:S(2)}) async-start(bf16[32,2,2880]{2,1,0:T(2,128)(2,1)} %reshape.104), calls=%async_computation.2 | async-start | bytes 753664 | tf_op jit(solution)/shard_map/all_to_all | solution.py:97
  151.8 0.2 convolution_add_fusion
  152.0 27.5 %reduce-scatter.5.cloned.1.call-done = bf16[64,2880]{1,0:T(8,128)(2,1)} async-done(((bf16[512,2880]{1,0:T(8,128)(2,1)}), bf16[64,2880]{1,0:T(8,128)(2,1)}) %reduce-scatter.5.cloned.1.call-update) | async-done | bytes 368656 | tf_op jit(solution)/shard_map/reduce_scatter | solution.py:95
  179.5 1.9 reshape.106
  181.3 10.0 %all-to-all-start.3 = ((bf16[32,2,2880]{2,1,0:T(2,128)(2,1)}), bf16[32,2,2880]{2,1,0:T(2,128)(2,1)S(1)}, u32[]{:S(2)}, u32[]{:S(2)}) async-start(bf16[32,2,2880]{2,1,0:T(2,128)(2,1)} %reshape.106), calls=%async_computation.5 | async-start | bytes 753664 | tf_op jit(solution)/shard_map/all_to_all | solution.py:97
  191.3 0.2 select_reduce_fusion.2
  191.5 0.1 copy.18
  191.6 0.1 mul.84
  191.7 0.1 copy.14
  191.8 10.6 %all-to-all-done.3 = bf16[32,2,2880]{2,1,0:T(2,128)(2,1)S(1)} async-done(((bf16[32,2,2880]{2,1,0:T(2,128)(2,1)}), bf16[32,2,2880]{2,1,0:T(2,128)(2,1)S(1)}, u32[]{:S(2)}, u32[]{:S(2)}) %all-to-all-start.3) | async-done | bytes 368672 | tf_op jit(solution)/shard_map/all_to_all | solution.py:97
  202.4 1.8 add_convert_fusion
  204.1 1.6 convert_element_type.63
  205.7 0.8 gather_fusion
  206.5 0.2 reshape.107
  206.7 1.2 multiply_reduce_fusion
  (25 shorter events, 0.1 us)
Async XLA Ops:
  6.5 64.4 %copy-start = (bf16[1,360,2880]{2,1,0:T(8,128)(2,1)S(1)}, bf16[1,360,2880]{2,1,0:T(8,128)(2,1)}, u32[]{:S(2)}) copy-start(bf16[1,360,2880]{2,1,0:T(8,128)(2,1)} %param.18) | copy-start | bytes 6220804
  6.5 60.5 %all-gather.3.cloned.1.call-start = ((), (), s32[]{:S(2)}) async-start(), calls=%async_computation.6 | async-start | bytes 3391488 | tf_op jit(solution)/shard_map/all_gather | solution.py:88
  13.7 46.3 %copy-start.5 = (f32[1,2,360]{2,1,0:T(2,128)S(1)}, f32[1,2,360]{2,1,0:T(2,128)}, u32[]{:S(2)}) copy-start(f32[1,2,360]{2,1,0:T(2,128)} %param.17) | copy-start | bytes 8644
  40.5 58.3 %all-gather.5.cloned.1.call-start = ((), (), s32[]{:S(2)}) async-start(), calls=%async_computation.8 | async-start | bytes 3391488 | tf_op jit(solution)/shard_map/all_gather | solution.py:88
  59.9 79.8 %reduce-scatter.3.cloned.1.call-start = ((), (), s32[]{:S(2)}) async-start(), calls=%async_computation.7 | async-start | bytes 3391488 | tf_op jit(solution)/shard_map/reduce_scatter | solution.py:95
  78.4 101.1 %reduce-scatter.5.cloned.1.call-start = ((), (), s32[]{:S(2)}) async-start(), calls=%async_computation.9 | async-start | bytes 3391488 | tf_op jit(solution)/shard_map/reduce_scatter | solution.py:95
  110.1 41.7 %copy-start.2 = (bf16[16,2880]{1,0:T(8,128)(2,1)S(1)}, bf16[16,2880]{1,0:T(8,128)(2,1)}, u32[]{:S(2)}) copy-start(bf16[16,2880]{1,0:T(8,128)(2,1)} %param.10) | copy-start | bytes 276484
  110.1 41.7 %copy-start.3 = (f32[2880]{0:T(1024)S(1)}, f32[2880]{0:T(1024)}, u32[]{:S(2)}) copy-start(f32[2880]{0:T(1024)} %param.11) | copy-start | bytes 34564
  110.1 41.7 %copy-start.6 = (bf16[2880,32]{0,1:T(8,128)(2,1)S(1)}, bf16[2880,32]{0,1:T(8,128)(2,1)}, u32[]{:S(2)}) copy-start(bf16[2880,32]{0,1:T(8,128)(2,1)} %param.12) | copy-start | bytes 552964
  110.1 41.7 %copy-start.7 = (f32[32]{0:T(128)S(1)}, f32[32]{0:T(128)}, u32[]{:S(2)}) copy-start(f32[32]{0:T(128)} %param.13) | copy-start | bytes 388
  110.1 81.3 %copy-start.4 = (s32[16,4]{0,1:T(4,128)S(1)}, s32[16,4]{0,1:T(4,128)}, u32[]{:S(2)}) copy-start(s32[16,4]{0,1:T(4,128)} %param.14) | copy-start | bytes 772
  110.1 92.3 %copy-start.1 = (f32[32,2880]{1,0:T(8,128)S(1)}, f32[32,2880]{1,0:T(8,128)}, u32[]{:S(2)}) copy-start(f32[32,2880]{1,0:T(8,128)} %param.19) | copy-start | bytes 1105924
  141.6 39.7 %all-to-all-start.1 = ((bf16[32,2,2880]{2,1,0:T(2,128)(2,1)}), bf16[32,2,2880]{2,1,0:T(2,128)(2,1)S(1)}, u32[]{:S(2)}, u32[]{:S(2)}) async-start(bf16[32,2,2880]{2,1,0:T(2,128)(2,1)} %reshape.104), calls=%async_computation.2 | async-start | bytes 753664 | tf_op jit(solution)/shard_map/all_to_all | solution.py:97
  181.3 21.0 %all-to-all-start.3 = ((bf16[32,2,2880]{2,1,0:T(2,128)(2,1)}), bf16[32,2,2880]{2,1,0:T(2,128)(2,1)S(1)}, u32[]{:S(2)}, u32[]{:S(2)}) async-start(bf16[32,2,2880]{2,1,0:T(2,128)(2,1)} %reshape.106), calls=%async_computation.5 | async-start | bytes 753664 | tf_op jit(solution)/shard_map/all_to_all | solution.py:97
Sparse Core Ops, SparseCore 0:
  40.6 26.4 all-gather.2
  68.9 29.8 all-gather.4
  101.4 38.3 reduce-scatter.2
  142.2 37.2 reduce-scatter.4

commit v5 on v3

--- a/solution.py
+++ b/solution.py
@@ -2,6 +2,7 @@
 import jax.numpy as jnp
 from jax import lax
 from jax.sharding import PartitionSpec as P
+from jax.experimental.layout import Layout, with_layout_constraint
 
 TOPK = 4
 
@@ -72,6 +73,7 @@
         (target_row[:, :, None] == targets[None, None, :]).astype(jnp.int32), axis=1
     ).astype(jnp.bfloat16)
     outgoing = jnp.dot(dispatch.T, normed, preferred_element_type=jnp.float32).astype(jnp.bfloat16)
+    outgoing = with_layout_constraint(outgoing, Layout(major_to_minor=(0, 1)))
     outgoing = outgoing.reshape(experts, capacity, model_width)
     gate_weight = gate_up[0, 0]
     up_weight = gate_up[0, 1]
@@ -86,6 +88,7 @@
     up_value = jnp.dot(flat_rows, up_weight, preferred_element_type=jnp.float32) + up_bias
     hidden = swiglu(gate_value, up_value).astype(jnp.bfloat16)
     partials = jnp.dot(hidden, down_weight, preferred_element_type=jnp.float32).astype(jnp.bfloat16)
+    partials = with_layout_constraint(partials, Layout(major_to_minor=(0, 1)))
     reduced_parts = lax.psum_scatter(partials, "dp", scatter_dimension=0, tiled=True)
     reduced_parts = reduced_parts.reshape(expert_count, capacity, model_width)
     reduced = lax.all_to_all(reduced_parts, "expert", split_axis=0, concat_axis=0, tiled=True)

time: 203 us -> 194 us (0.956)
  local copies, waits for them, and re-layouts: 17.8 us -> 7.86 us
    unnamed x17 -> x14, local copies, waits for them, and re-layouts: 8.55 us -> 0.05 us
    dot_general x1, matrix products: 5.2 us -> 10.9 us  [body(): jnp.dot(hidden, down_weight, preferred_element_type=jnp.float32)]
    dot_general x1 -> x0, matrix products: 4.44 us -> none  [body(): jnp.dot(flat_rows, up_weight, preferred_element_type=jnp.float32) + up_bias]
where the time goes in v5:
time: 194 us; the launch traced here: 193 us
  waiting for transfers between devices  103 us (53%)
  blocking collectives  33.4 us (17%)
  matrix products  20.3 us (10%)
  between operations  13.6 us (7%)
  starting transfers between devices  10.2 us (5%)
  local copies, waits for them, and re-layouts  7.86 us (4%)
  other arithmetic  5.2 us (3%)
    reduce_scatter x1, waiting for transfers between devices, body(): lax.psum_scatter(partials, 'dp', scatter_dimension=0, tiled=True)  44.2 us
    all_gather x1, waiting for transfers between devices, body(): flat_rows = lax.all_gather(row_block, 'dp', axis=0, tiled=True)  39.1 us
    all_to_all x1, blocking collectives, body(): lax.all_to_all(outgoing, 'expert', split_axis=0, concat_axis=0, tiled=True)  33.4 us
    all_to_all x1, waiting for transfers between devices, body(): lax.all_to_all(reduced_parts, 'expert', split_axis=0, concat_axis=0, tile...  19.3 us
    dot_general x1, matrix products, body(): jnp.dot(hidden, down_weight, preferred_element_type=jnp.float32)  10.9 us
    all_to_all x1, starting transfers between devices, body(): lax.all_to_all(reduced_parts, 'expert', split_axis=0, concat_axis=0, tile...  10.2 us
    dot_general x1, matrix products, body(): jnp.dot(flat_rows, gate_weight, preferred_element_type=jnp.float32)  7.04 us
  transfers between devices with their start and end apart: 3, of which 3 were waited for; matrix products, arithmetic and copies ran while one was open for 1% of the time, Pallas kernels for 0%

profile of v5, /device:TPU:8, one launch (start us, length us, event | category | flops | bytes accessed | tf_op | source)
XLA Modules:
  0.0 193.2 jit_solution(8038303960669636335)
XLA Ops:
  6.5 0.0 copy-start
  6.5 0.0 all-gather.2.cloned.1.call-start
  6.5 1.1 select_reduce_fusion.1
  7.6 0.1 copy.14
  7.7 0.1 eq.23
  7.8 0.1 fusion.14
  7.9 0.1 reduce_window_sum.11
  8.0 0.2 select_reduce_fusion
  8.1 0.1 reshape.92
  8.2 0.1 copy.15
  8.3 0.1 convert_reduce_fusion
  8.4 1.0 fusion.11
  9.5 1.3 convolution_convert_fusion.1
  10.8 1.0 reshape.93
  11.8 33.4 %all_to_all.10 = bf16[32,4,2880]{2,1,0:T(4,128)(2,1)S(1)} all-to-all(bf16[32,4,2880]{2,1,0:T(4,128)(2,1)} %reshape.93), channel_id=1, replica_groups=mesh['dp'=8,'expert'=32] {'expert'}, dimensions={0} | all-to-all | bytes 1474560 | tf_op jit(solution)/shard_map/all_to_all | solution.py:84
  45.3 1.2 reshape.94
  46.5 0.0 all-gather.2.cloned.1.call-update
  46.5 0.0 reduce-scatter.2.cloned.1.call-start
  46.6 0.0 copy-done.5
  46.6 39.1 %all-gather.2.cloned.1.call-done = bf16[1024,2880]{1,0:T(8,128)(2,1)} async-done(((bf16[128,2880]{1,0:T(8,128)(2,1)}), bf16[1024,2880]{1,0:T(8,128)(2,1)}) %all-gather.2.cloned.1.call-update) | async-done | bytes 5898256 | tf_op jit(solution)/shard_map/all_gather | solution.py:86
  85.7 7.0 %fusion.1 = f32[1024,360]{0,1:T(8,128)} fusion(bf16[1024,2880]{1,0:T(8,128)(2,1)} %all-gather.2.cloned.1.call-done, bf16[1,2,2880,360]{2,3,1,0:T(8,128)(2,1)} %param.16), kind=kOutput, calls=%fused_computation.4 | convolution fusion | flops 2123366400 | bytes 9623552 | tf_op jit(solution)/shard_map/dot_general | solution.py:87
  92.7 0.0 copy-done
  92.7 10.9 %convolution_convert_fusion = bf16[1024,2880]{1,0:T(8,128)(2,1)} fusion(bf16[1,360,2880]{2,1,0:T(8,128)(2,1)S(1)} %copy-done, f32[1024,360]{0,1:T(8,128)} %fusion.1, bf16[1024,2880]{1,0:T(8,128)(2,1)} %all-gather.2.cloned.1.call-done, bf16[1,2,2880,360]{2,3,1,0:T(8,128)(2,1)} %param.16, f32[360]{0:T(512)S(1)} %get-tuple-element.6, f32[360]{0:T(512)S(1)} %get-tuple-element.5), kind=kOutput, calls=%fused_computation.1 | convolution fusion | flops 4254105600 | bytes 17598272 | tf_op jit(solution)/shard_map/dot_general | solution.py:90
  103.6 0.0 reduce-scatter.2.cloned.1.call-update
  103.6 0.0 copy-start.2
  103.6 0.0 copy-start.3
  103.6 0.0 copy-start.6
  103.7 0.0 copy-start.4
  103.7 0.0 copy-start.1
  103.7 44.2 %reduce-scatter.2.cloned.1.call-done = bf16[128,2880]{1,0:T(8,128)(2,1)} async-done(((bf16[1024,2880]{1,0:T(8,128)(2,1)}), bf16[128,2880]{1,0:T(8,128)(2,1)}) %reduce-scatter.2.cloned.1.call-update) | async-done | bytes 737296 | tf_op jit(solution)/shard_map/reduce_scatter | solution.py:92
  147.9 2.4 %reshape.95 = bf16[32,4,2880]{2,1,0:T(4,128)(2,1)} reshape(bf16[128,2880]{1,0:T(8,128)(2,1)} %reduce-scatter.2.cloned.1.call-done) | data formatting | bytes 1474560 | tf_op jit(solution)/shard_map/reshape | solution.py:93
  150.3 10.2 %all-to-all-start.1 = ((bf16[32,4,2880]{2,1,0:T(4,128)(2,1)}), bf16[32,4,2880]{2,1,0:T(4,128)(2,1)S(1)}, u32[]{:S(2)}, u32[]{:S(2)}) async-start(bf16[32,4,2880]{2,1,0:T(4,128)(2,1)} %reshape.95), calls=%async_computation.2 | async-start | bytes 1507328 | tf_op jit(solution)/shard_map/all_to_all | solution.py:94
  160.5 0.1 copy.16
  160.5 0.1 mul.76
  160.6 0.0 copy-done.2
  160.6 0.0 copy-done.3
  160.7 0.0 copy-done.6
  160.7 1.1 convolution_add_fusion
  161.8 0.0 copy-done.4
  161.8 0.2 select_reduce_fusion.2
  162.0 0.1 copy.13
  162.1 19.3 %all-to-all-done.1 = bf16[32,4,2880]{2,1,0:T(4,128)(2,1)S(1)} async-done(((bf16[32,4,2880]{2,1,0:T(4,128)(2,1)}), bf16[32,4,2880]{2,1,0:T(4,128)(2,1)S(1)}, u32[]{:S(2)}, u32[]{:S(2)}) %all-to-all-start.1) | async-done | bytes 737312 | tf_op jit(solution)/shard_map/all_to_all | solution.py:94
  181.4 0.0 copy-done.1
  181.4 1.3 add_convert_fusion
  182.7 1.6 reshape.96
  184.2 0.8 gather_fusion
  185.0 0.2 reshape.97
  185.2 1.2 multiply_reduce_fusion
  (8 shorter events, 0.1 us)
Async XLA Ops:
  6.5 86.2 %copy-start = (bf16[1,360,2880]{2,1,0:T(8,128)(2,1)S(1)}, bf16[1,360,2880]{2,1,0:T(8,128)(2,1)}, u32[]{:S(2)}) copy-start(bf16[1,360,2880]{2,1,0:T(8,128)(2,1)} %param.18) | copy-start | bytes 6220804
  6.5 79.2 %all-gather.2.cloned.1.call-start = ((), (), s32[]{:S(2)}) async-start(), calls=%async_computation.3 | async-start | bytes 6782976 | tf_op jit(solution)/shard_map/all_gather | solution.py:86
  45.3 1.3 copy-start.5
  46.5 101.4 %reduce-scatter.2.cloned.1.call-start = ((), (), s32[]{:S(2)}) async-start(), calls=%async_computation.4 | async-start | bytes 6782976 | tf_op jit(solution)/shard_map/reduce_scatter | solution.py:92
  103.6 57.0 %copy-start.2 = (bf16[16,2880]{1,0:T(8,128)(2,1)S(1)}, bf16[16,2880]{1,0:T(8,128)(2,1)}, u32[]{:S(2)}) copy-start(bf16[16,2880]{1,0:T(8,128)(2,1)} %param.10) | copy-start | bytes 276484
  103.6 57.0 %copy-start.3 = (f32[2880]{0:T(1024)S(1)}, f32[2880]{0:T(1024)}, u32[]{:S(2)}) copy-start(f32[2880]{0:T(1024)} %param.11) | copy-start | bytes 34564
  103.6 57.0 %copy-start.6 = (f32[32]{0:T(128)S(1)}, f32[32]{0:T(128)}, u32[]{:S(2)}) copy-start(f32[32]{0:T(128)} %param.13) | copy-start | bytes 388
  103.7 58.2 %copy-start.4 = (s32[16,4]{0,1:T(4,128)S(1)}, s32[16,4]{0,1:T(4,128)}, u32[]{:S(2)}) copy-start(s32[16,4]{0,1:T(4,128)} %param.14) | copy-start | bytes 772
  103.7 77.7 %copy-start.1 = (f32[32,2880]{1,0:T(8,128)S(1)}, f32[32,2880]{1,0:T(8,128)}, u32[]{:S(2)}) copy-start(f32[32,2880]{1,0:T(8,128)} %param.19) | copy-start | bytes 1105924
  150.3 31.1 %all-to-all-start.1 = ((bf16[32,4,2880]{2,1,0:T(4,128)(2,1)}), bf16[32,4,2880]{2,1,0:T(4,128)(2,1)S(1)}, u32[]{:S(2)}, u32[]{:S(2)}) async-start(bf16[32,4,2880]{2,1,0:T(4,128)(2,1)} %reshape.95), calls=%async_computation.2 | async-start | bytes 1507328 | tf_op jit(solution)/shard_map/all_to_all | solution.py:94
Sparse Core Ops, SparseCore 0:
  46.6 39.0 all-gather.1
  103.7 44.1 reduce-scatter.1

commit v6 on v5

--- a/solution.py
+++ b/solution.py
@@ -64,6 +64,7 @@
     experts = placement.shape[0]
     capacity = max(2, 2 * tok_dev * TOPK // experts)
     expert_count = lax.axis_size("expert")
+    dp_count = lax.axis_size("dp")
     normed = normalize(tokens, norm_gain)
     weights = routing(normed, router_weight, router_bias, expert_ids)
     columns = lookup(expert_ids, placement)
@@ -87,8 +88,11 @@
     gate_value = jnp.dot(flat_rows, gate_weight, preferred_element_type=jnp.float32) + gate_bias
     up_value = jnp.dot(flat_rows, up_weight, preferred_element_type=jnp.float32) + up_bias
     hidden = swiglu(gate_value, up_value).astype(jnp.bfloat16)
-    partials = jnp.dot(hidden, down_weight, preferred_element_type=jnp.float32).astype(jnp.bfloat16)
-    partials = with_layout_constraint(partials, Layout(major_to_minor=(0, 1)))
+    hidden = hidden.reshape(dp_count, -1, hidden.shape[-1])
+    partials = jnp.einsum("grf,fo->gro", hidden, down_weight, preferred_element_type=jnp.float32)
+    partials = partials.astype(jnp.bfloat16)
+    partials = with_layout_constraint(partials, Layout(major_to_minor=(0, 1, 2)))
+    partials = partials.reshape(-1, model_width)
     reduced_parts = lax.psum_scatter(partials, "dp", scatter_dimension=0, tiled=True)
     reduced_parts = reduced_parts.reshape(expert_count, capacity, model_width)
     reduced = lax.all_to_all(reduced_parts, "expert", split_axis=0, concat_axis=0, tiled=True)

time: 194 us -> 192 us (0.990)
  matrix products: 20.3 us -> 18.3 us
    dot_general x1 -> x2, matrix products: 10.9 us -> 9.87 us  [the longest x1 5.42 us: body(): jnp.einsum('grf,fo->gro', hidden, down_weight, preferred_element_type=jnp...]
where the time goes in v6:
time: 192 us; the launch traced here: 191 us
  waiting for transfers between devices  103 us (54%)
  blocking collectives  33.4 us (17%)
  matrix products  18.3 us (10%)
  between operations  13.6 us (7%)
  starting transfers between devices  10.2 us (5%)
  local copies, waits for them, and re-layouts  7.85 us (4%)
  other arithmetic  5.2 us (3%)
    reduce_scatter x1, waiting for transfers between devices, body(): lax.psum_scatter(partials, 'dp', scatter_dimension=0, tiled=True)  44.2 us
    all_gather x1, waiting for transfers between devices, body(): flat_rows = lax.all_gather(row_block, 'dp', axis=0, tiled=True)  39.1 us
    all_to_all x1, blocking collectives, body(): lax.all_to_all(outgoing, 'expert', split_axis=0, concat_axis=0, tiled=True)  33.4 us
    all_to_all x1, waiting for transfers between devices, body(): lax.all_to_all(reduced_parts, 'expert', split_axis=0, concat_axis=0, tile...  19.3 us
    all_to_all x1, starting transfers between devices, body(): lax.all_to_all(reduced_parts, 'expert', split_axis=0, concat_axis=0, tile...  10.2 us
    dot_general x1, matrix products, body(): jnp.dot(flat_rows, gate_weight, preferred_element_type=jnp.float32)  5.98 us
    dot_general x1, matrix products, body(): jnp.einsum('grf,fo->gro', hidden, down_weight, preferred_element_type=jnp...  5.42 us
    dot_general x1, matrix products, body(): jnp.dot(flat_rows, up_weight, preferred_element_type=jnp.float32) + up_bias  4.45 us
  transfers between devices with their start and end apart: 3, of which 3 were waited for; matrix products, arithmetic and copies ran while one was open for 1% of the time, Pallas kernels for 0%

profile of v6, /device:TPU:8, one launch (start us, length us, event | category | flops | bytes accessed | tf_op | source)
XLA Modules:
  0.0 191.2 jit_solution(17139302259608479190)
XLA Ops:
  6.5 0.0 copy-start
  6.5 0.0 all-gather.2.cloned.1.call-start
  6.5 1.1 select_reduce_fusion.1
  7.6 0.1 copy.16
  7.7 0.1 eq.23
  7.8 0.1 fusion.17
  7.9 0.1 reduce_window_sum.11
  8.0 0.2 select_reduce_fusion
  8.1 0.1 reshape.98
  8.2 0.1 copy.17
  8.3 0.1 convert_reduce_fusion
  8.4 1.0 fusion.14
  9.5 1.3 convolution_convert_fusion.1
  10.8 1.0 reshape.99
  11.8 33.4 %all_to_all.10 = bf16[32,4,2880]{2,1,0:T(4,128)(2,1)S(1)} all-to-all(bf16[32,4,2880]{2,1,0:T(4,128)(2,1)} %reshape.99), channel_id=1, replica_groups=mesh['dp'=8,'expert'=32] {'expert'}, dimensions={0} | all-to-all | bytes 1474560 | tf_op jit(solution)/shard_map/all_to_all | solution.py:85
  45.3 1.2 reshape.100
  46.5 0.0 all-gather.2.cloned.1.call-update
  46.5 0.0 reduce-scatter.2.cloned.1.call-start
  46.6 0.0 copy-done.5
  46.6 39.1 %all-gather.2.cloned.1.call-done = bf16[1024,2880]{1,0:T(8,128)(2,1)} async-done(((bf16[128,2880]{1,0:T(8,128)(2,1)}), bf16[1024,2880]{1,0:T(8,128)(2,1)}) %all-gather.2.cloned.1.call-update) | async-done | bytes 5898256 | tf_op jit(solution)/shard_map/all_gather | solution.py:87
  85.7 6.0 %fusion.1 = f32[1024,360]{0,1:T(8,128)S(1)} fusion(bf16[1024,2880]{1,0:T(8,128)(2,1)} %all-gather.2.cloned.1.call-done, bf16[1,2,2880,360]{2,3,1,0:T(8,128)(2,1)} %param.16), kind=kOutput, calls=%fused_computation.4 | convolution fusion | flops 2123366400 | bytes 9623552 | tf_op jit(solution)/shard_map/dot_general | solution.py:88
  91.7 0.0 copy-done.6
  91.7 4.4 %fusion.9 = bf16[45,8,8,128]{3,2,1,0:T(8,128)(2,1)S(1)} fusion(f32[1024,360]{0,1:T(8,128)S(1)} %fusion.1, bf16[1024,2880]{1,0:T(8,128)(2,1)S(1)} %copy-done.6, bf16[1,2,2880,360]{2,3,1,0:T(8,128)(2,1)} %param.16, f32[360]{0:T(512)S(1)} %get-tuple-element.6, f32[360]{0:T(512)S(1)} %get-tuple-element.5), kind=kOutput, calls=%fused_computation.12 | convolution fusion | flops 2127790080 | bytes 10232640 | tf_op jit(solution)/shard_map/dot_general | solution.py:89
  96.2 5.4 %convolution_convert_fusion = bf16[8,128,2880]{2,1,0:T(8,128)(2,1)} fusion(bf16[1,360,2880]{2,1,0:T(8,128)(2,1)S(1)} %copy-done, bf16[45,8,8,128]{3,2,1,0:T(8,128)(2,1)S(1)} %fusion.9), kind=kOutput, calls=%fused_computation.1 | convolution fusion | flops 2126315520 | bytes 8709120 | tf_op jit(solution)/shard_map/grf,fo->gro/dot_general | solution.py:92
  101.6 0.0 reduce-scatter.2.cloned.1.call-update
  101.6 0.0 copy-start.2
  101.6 0.0 copy-start.3
  101.6 0.0 copy-start.7
  101.6 0.0 copy-start.4
  101.6 0.0 copy-start.1
  101.7 44.2 %reduce-scatter.2.cloned.1.call-done = bf16[128,2880]{1,0:T(8,128)(2,1)} async-done(((bf16[1024,2880]{1,0:T(8,128)(2,1)}), bf16[128,2880]{1,0:T(8,128)(2,1)}) %reduce-scatter.2.cloned.1.call-update) | async-done | bytes 737296 | tf_op jit(solution)/shard_map/reduce_scatter | solution.py:96
  145.9 2.4 %reshape.103 = bf16[32,4,2880]{2,1,0:T(4,128)(2,1)} reshape(bf16[128,2880]{1,0:T(8,128)(2,1)} %reduce-scatter.2.cloned.1.call-done) | data formatting | bytes 1474560 | tf_op jit(solution)/shard_map/reshape | solution.py:97
  148.3 10.2 %all-to-all-start.1 = ((bf16[32,4,2880]{2,1,0:T(4,128)(2,1)}), bf16[32,4,2880]{2,1,0:T(4,128)(2,1)S(1)}, u32[]{:S(2)}, u32[]{:S(2)}) async-start(bf16[32,4,2880]{2,1,0:T(4,128)(2,1)} %reshape.103), calls=%async_computation.2 | async-start | bytes 1507328 | tf_op jit(solution)/shard_map/all_to_all | solution.py:98
  158.4 0.1 copy.19
  158.5 0.1 mul.76
  158.6 0.0 copy-done.2
  158.6 0.0 copy-done.3
  158.6 0.0 copy-done.7
  158.6 1.1 convolution_add_fusion
  159.8 0.0 copy-done.4
  159.8 0.2 select_reduce_fusion.2
  160.0 0.1 copy.15
  160.1 19.3 %all-to-all-done.1 = bf16[32,4,2880]{2,1,0:T(4,128)(2,1)S(1)} async-done(((bf16[32,4,2880]{2,1,0:T(4,128)(2,1)}), bf16[32,4,2880]{2,1,0:T(4,128)(2,1)S(1)}, u32[]{:S(2)}, u32[]{:S(2)}) %all-to-all-start.1) | async-done | bytes 737312 | tf_op jit(solution)/shard_map/all_to_all | solution.py:98
  179.4 1.3 add_convert_fusion
  180.6 1.6 reshape.104
  182.2 0.8 gather_fusion
  183.0 0.2 reshape.105
  183.2 1.2 multiply_reduce_fusion
  (11 shorter events, 0.1 us)
Async XLA Ops:
  6.5 89.6 %copy-start = (bf16[1,360,2880]{2,1,0:T(8,128)(2,1)S(1)}, bf16[1,360,2880]{2,1,0:T(8,128)(2,1)}, u32[]{:S(2)}) copy-start(bf16[1,360,2880]{2,1,0:T(8,128)(2,1)} %param.18) | copy-start | bytes 6220804
  6.5 79.2 %all-gather.2.cloned.1.call-start = ((), (), s32[]{:S(2)}) async-start(), calls=%async_computation.3 | async-start | bytes 6782976 | tf_op jit(solution)/shard_map/all_gather | solution.py:87
  45.3 1.3 copy-start.5
  46.5 99.4 %reduce-scatter.2.cloned.1.call-start = ((), (), s32[]{:S(2)}) async-start(), calls=%async_computation.4 | async-start | bytes 6782976 | tf_op jit(solution)/shard_map/reduce_scatter | solution.py:96
  85.7 6.0 %copy-start.6 = (bf16[1024,2880]{1,0:T(8,128)(2,1)S(1)}, bf16[1024,2880]{1,0:T(8,128)(2,1)}, u32[]{:S(2)}) copy-start(bf16[1024,2880]{1,0:T(8,128)(2,1)} %all-gather.2.cloned.1.call-done) | copy-start | bytes 17694724
  101.6 57.0 %copy-start.2 = (bf16[16,2880]{1,0:T(8,128)(2,1)S(1)}, bf16[16,2880]{1,0:T(8,128)(2,1)}, u32[]{:S(2)}) copy-start(bf16[16,2880]{1,0:T(8,128)(2,1)} %param.10) | copy-start | bytes 276484
  101.6 57.0 %copy-start.3 = (f32[2880]{0:T(1024)S(1)}, f32[2880]{0:T(1024)}, u32[]{:S(2)}) copy-start(f32[2880]{0:T(1024)} %param.11) | copy-start | bytes 34564
  101.6 57.0 %copy-start.7 = (f32[32]{0:T(128)S(1)}, f32[32]{0:T(128)}, u32[]{:S(2)}) copy-start(f32[32]{0:T(128)} %param.13) | copy-start | bytes 388
  101.6 58.2 %copy-start.4 = (s32[16,4]{0,1:T(4,128)S(1)}, s32[16,4]{0,1:T(4,128)}, u32[]{:S(2)}) copy-start(s32[16,4]{0,1:T(4,128)} %param.14) | copy-start | bytes 772
  101.6 77.7 %copy-start.1 = (f32[32,2880]{1,0:T(8,128)S(1)}, f32[32,2880]{1,0:T(8,128)}, u32[]{:S(2)}) copy-start(f32[32,2880]{1,0:T(8,128)} %param.19) | copy-start | bytes 1105924
  148.3 31.1 %all-to-all-start.1 = ((bf16[32,4,2880]{2,1,0:T(4,128)(2,1)}), bf16[32,4,2880]{2,1,0:T(4,128)(2,1)S(1)}, u32[]{:S(2)}, u32[]{:S(2)}) async-start(bf16[32,4,2880]{2,1,0:T(4,128)(2,1)} %reshape.103), calls=%async_computation.2 | async-start | bytes 1507328 | tf_op jit(solution)/shard_map/all_to_all | solution.py:98
Sparse Core Ops, SparseCore 0:
  46.6 39.0 all-gather.1
  101.7 44.1 reduce-scatter.1

commit v7 on v6

--- a/solution.py
+++ b/solution.py
@@ -68,7 +68,8 @@
     normed = normalize(tokens, norm_gain)
     weights = routing(normed, router_weight, router_bias, expert_ids)
     columns = lookup(expert_ids, placement)
-    target_row = columns * capacity + slot_positions(columns, experts)
+    slots = slot_positions(columns, experts)
+    target_row = columns * capacity + slots
     targets = jnp.arange(experts * capacity, dtype=jnp.int32)
     dispatch = jnp.sum(
         (target_row[:, :, None] == targets[None, None, :]).astype(jnp.int32), axis=1
@@ -98,9 +99,9 @@
     reduced = lax.all_to_all(reduced_parts, "expert", split_axis=0, concat_axis=0, tiled=True)
     reduced = reduced.astype(jnp.float32)
     reduced = reduced.reshape(experts, capacity, model_width) + down_bias[:, None, :]
-    returned = reduced.astype(jnp.bfloat16).reshape(experts * capacity, model_width)
+    returned = reduced.astype(jnp.bfloat16)
     picked = (
-        returned[target_row.reshape(-1)].reshape(tok_dev, TOPK, model_width).astype(jnp.float32)
+        returned[columns, slots].astype(jnp.float32)
     )
     return jnp.sum(weights[:, :, None] * picked, axis=1).astype(jnp.bfloat16)
 

time: 192 us -> 191 us (level)
  transfers between devices with their start and end apart: 3 -> 3, of which waited for: 3 -> 3; matrix products, arithmetic and copies ran while one was open for 1% -> 0% of each run, Pallas kernels for 0% -> 0%
where the time goes in v7:
time: 191 us
  waiting for transfers between devices  103 us (54%)
  blocking collectives  33.4 us (17%)
  matrix products  17.4 us (9%)
  between operations  13.6 us (7%)
  starting transfers between devices  10.2 us (5%)
  local copies, waits for them, and re-layouts  7.47 us (4%)
  other arithmetic  5.47 us (3%)
    reduce_scatter x1, waiting for transfers between devices, body(): lax.psum_scatter(partials, 'dp', scatter_dimension=0, tiled=True)  44.2 us
    all_gather x1, waiting for transfers between devices, body(): flat_rows = lax.all_gather(row_block, 'dp', axis=0, tiled=True)  39.1 us
    all_to_all x1, blocking collectives, body(): lax.all_to_all(outgoing, 'expert', split_axis=0, concat_axis=0, tiled=True)  33.4 us
    all_to_all x1, waiting for transfers between devices, body(): lax.all_to_all(reduced_parts, 'expert', split_axis=0, concat_axis=0, tile...  20.1 us
    all_to_all x1, starting transfers between devices, body(): lax.all_to_all(reduced_parts, 'expert', split_axis=0, concat_axis=0, tile...  10.2 us
    dot_general x1, matrix products, body(): jnp.dot(flat_rows, gate_weight, preferred_element_type=jnp.float32)  5.98 us
    dot_general x1, matrix products, body(): jnp.einsum('grf,fo->gro', hidden, down_weight, preferred_element_type=jnp...  5.42 us
    dot_general x1, matrix products, body(): jnp.dot(flat_rows, up_weight, preferred_element_type=jnp.float32) + up_bias  4.45 us
  transfers between devices with their start and end apart: 3, of which 3 were waited for; matrix products, arithmetic and copies ran while one was open for 0% of the time, Pallas kernels for 0%

profile of v7, /device:TPU:8, one launch (start us, length us, event | category | flops | bytes accessed | tf_op | source)
XLA Modules:
  0.0 191.0 jit_solution(18311879708302291649)
XLA Ops:
  6.5 0.0 copy-start
  6.5 0.0 all-gather.2.cloned.1.call-start
  6.5 1.1 select_reduce_fusion.1
  7.6 0.1 copy.26
  7.7 0.1 eq.23
  7.8 0.1 fusion.17
  7.9 0.1 reduce_window_sum.11
  8.0 0.2 select_reduce_fusion
  8.1 0.1 reshape.105
  8.2 0.1 copy.27
  8.3 0.1 convert_reduce_fusion
  8.4 1.0 fusion.14
  9.5 1.3 convolution_convert_fusion.1
  10.8 1.0 reshape.106
  11.8 33.4 %all_to_all.10 = bf16[32,4,2880]{2,1,0:T(4,128)(2,1)S(1)} all-to-all(bf16[32,4,2880]{2,1,0:T(4,128)(2,1)} %reshape.106), channel_id=1, replica_groups=mesh['dp'=8,'expert'=32] {'expert'}, dimensions={0} | all-to-all | bytes 1474560 | tf_op jit(solution)/shard_map/all_to_all | solution.py:86
  45.3 1.2 reshape.107
  46.5 0.0 all-gather.2.cloned.1.call-update
  46.5 0.0 reduce-scatter.2.cloned.1.call-start
  46.6 39.1 %all-gather.2.cloned.1.call-done = bf16[1024,2880]{1,0:T(8,128)(2,1)} async-done(((bf16[128,2880]{1,0:T(8,128)(2,1)}), bf16[1024,2880]{1,0:T(8,128)(2,1)}) %all-gather.2.cloned.1.call-update) | async-done | bytes 5898256 | tf_op jit(solution)/shard_map/all_gather | solution.py:88
  85.7 6.0 %fusion.1 = f32[1024,360]{0,1:T(8,128)S(1)} fusion(bf16[1024,2880]{1,0:T(8,128)(2,1)} %all-gather.2.cloned.1.call-done, bf16[1,2,2880,360]{2,3,1,0:T(8,128)(2,1)} %param.16), kind=kOutput, calls=%fused_computation.4 | convolution fusion | flops 2123366400 | bytes 9623552 | tf_op jit(solution)/shard_map/dot_general | solution.py:89
  91.7 4.4 %fusion.9 = bf16[45,8,8,128]{3,2,1,0:T(8,128)(2,1)S(1)} fusion(f32[1024,360]{0,1:T(8,128)S(1)} %fusion.1, bf16[1024,2880]{1,0:T(8,128)(2,1)S(1)} %copy-done.6, bf16[1,2,2880,360]{2,3,1,0:T(8,128)(2,1)} %param.16, f32[360]{0:T(512)S(1)} %get-tuple-element.6, f32[360]{0:T(512)S(1)} %get-tuple-element.5), kind=kOutput, calls=%fused_computation.12 | convolution fusion | flops 2127790080 | bytes 10232640 | tf_op jit(solution)/shard_map/dot_general | solution.py:90
  96.2 5.4 %convolution_convert_fusion = bf16[8,128,2880]{2,1,0:T(8,128)(2,1)} fusion(bf16[1,360,2880]{2,1,0:T(8,128)(2,1)S(1)} %copy-done, bf16[45,8,8,128]{3,2,1,0:T(8,128)(2,1)S(1)} %fusion.9), kind=kOutput, calls=%fused_computation.1 | convolution fusion | flops 2126315520 | bytes 8709120 | tf_op jit(solution)/shard_map/grf,fo->gro/dot_general | solution.py:93
  101.6 0.0 reduce-scatter.2.cloned.1.call-update
  101.6 0.0 copy-start.2
  101.6 0.0 copy-start.3
  101.6 0.0 copy-start.7
  101.6 0.0 copy-start.8
  101.7 0.0 copy-start.4
  101.7 0.0 copy-start.1
  101.7 44.2 %reduce-scatter.2.cloned.1.call-done = bf16[128,2880]{1,0:T(8,128)(2,1)} async-done(((bf16[1024,2880]{1,0:T(8,128)(2,1)}), bf16[128,2880]{1,0:T(8,128)(2,1)}) %reduce-scatter.2.cloned.1.call-update) | async-done | bytes 737296 | tf_op jit(solution)/shard_map/reduce_scatter | solution.py:97
  145.9 2.4 %reshape.110 = bf16[32,4,2880]{2,1,0:T(4,128)(2,1)} reshape(bf16[128,2880]{1,0:T(8,128)(2,1)} %reduce-scatter.2.cloned.1.call-done) | data formatting | bytes 1474560 | tf_op jit(solution)/shard_map/reshape | solution.py:98
  148.3 10.2 %all-to-all-start.1 = ((bf16[32,4,2880]{2,1,0:T(4,128)(2,1)}), bf16[32,4,2880]{2,1,0:T(4,128)(2,1)}, u32[]{:S(2)}, u32[]{:S(2)}) async-start(bf16[32,4,2880]{2,1,0:T(4,128)(2,1)} %reshape.110), calls=%async_computation.2 | async-start | bytes 1507328 | tf_op jit(solution)/shard_map/all_to_all | solution.py:99
  158.5 0.1 reshape.111
  158.6 0.1 copy.29
  158.7 0.1 copy.32
  158.7 0.1 reshape.112
  158.8 0.0 copy-done.2
  158.8 0.0 copy-done.3
  158.9 0.0 copy-done.7
  158.9 0.0 copy-done.8
  158.9 0.2 convolution_add_fusion
  159.1 0.2 select_reduce_fusion.2
  159.3 0.1 copy.25
  159.4 20.1 %all-to-all-done.1 = bf16[32,4,2880]{2,1,0:T(4,128)(2,1)} async-done(((bf16[32,4,2880]{2,1,0:T(4,128)(2,1)}), bf16[32,4,2880]{2,1,0:T(4,128)(2,1)}, u32[]{:S(2)}, u32[]{:S(2)}) %all-to-all-start.1) | async-done | bytes 737312 | tf_op jit(solution)/shard_map/all_to_all | solution.py:99
  179.5 1.5 add_convert_fusion
  181.0 1.8 gather_fusion
  182.8 0.2 reshape.118
  183.0 1.2 multiply_reduce_fusion
  (13 shorter events, 0.1 us)
Async XLA Ops:
  6.5 89.6 %copy-start = (bf16[1,360,2880]{2,1,0:T(8,128)(2,1)S(1)}, bf16[1,360,2880]{2,1,0:T(8,128)(2,1)}, u32[]{:S(2)}) copy-start(bf16[1,360,2880]{2,1,0:T(8,128)(2,1)} %param.18) | copy-start | bytes 6220804
  6.5 79.2 %all-gather.2.cloned.1.call-start = ((), (), s32[]{:S(2)}) async-start(), calls=%async_computation.3 | async-start | bytes 6782976 | tf_op jit(solution)/shard_map/all_gather | solution.py:88
  45.3 1.3 copy-start.5
  46.5 99.4 %reduce-scatter.2.cloned.1.call-start = ((), (), s32[]{:S(2)}) async-start(), calls=%async_computation.4 | async-start | bytes 6782976 | tf_op jit(solution)/shard_map/reduce_scatter | solution.py:97
  85.7 6.0 %copy-start.6 = (bf16[1024,2880]{1,0:T(8,128)(2,1)S(1)}, bf16[1024,2880]{1,0:T(8,128)(2,1)}, u32[]{:S(2)}) copy-start(bf16[1024,2880]{1,0:T(8,128)(2,1)} %all-gather.2.cloned.1.call-done) | copy-start | bytes 17694724
  101.6 57.2 %copy-start.2 = (bf16[16,2880]{1,0:T(8,128)(2,1)S(1)}, bf16[16,2880]{1,0:T(8,128)(2,1)}, u32[]{:S(2)}) copy-start(bf16[16,2880]{1,0:T(8,128)(2,1)} %param.10) | copy-start | bytes 276484
  101.6 57.2 %copy-start.3 = (f32[2880]{0:T(1024)S(1)}, f32[2880]{0:T(1024)}, u32[]{:S(2)}) copy-start(f32[2880]{0:T(1024)} %param.11) | copy-start | bytes 34564
  101.6 57.2 %copy-start.7 = (bf16[2880,32]{0,1:T(8,128)(2,1)S(1)}, bf16[2880,32]{0,1:T(8,128)(2,1)}, u32[]{:S(2)}) copy-start(bf16[2880,32]{0,1:T(8,128)(2,1)} %param.12) | copy-start | bytes 552964
  101.6 57.2 %copy-start.8 = (f32[32]{0:T(128)S(1)}, f32[32]{0:T(128)}, u32[]{:S(2)}) copy-start(f32[32]{0:T(128)} %param.13) | copy-start | bytes 388
  101.7 57.5 %copy-start.4 = (s32[16,4]{0,1:T(4,128)S(1)}, s32[16,4]{0,1:T(4,128)}, u32[]{:S(2)}) copy-start(s32[16,4]{0,1:T(4,128)} %param.14) | copy-start | bytes 772
  101.7 77.8 %copy-start.1 = (f32[32,2880]{1,0:T(8,128)S(1)}, f32[32,2880]{1,0:T(8,128)}, u32[]{:S(2)}) copy-start(f32[32,2880]{1,0:T(8,128)} %param.19) | copy-start | bytes 1105924
  148.3 31.2 %all-to-all-start.1 = ((bf16[32,4,2880]{2,1,0:T(4,128)(2,1)}), bf16[32,4,2880]{2,1,0:T(4,128)(2,1)}, u32[]{:S(2)}, u32[]{:S(2)}) async-start(bf16[32,4,2880]{2,1,0:T(4,128)(2,1)} %reshape.110), calls=%async_computation.2 | async-start | bytes 1507328 | tf_op jit(solution)/shard_map/all_to_all | solution.py:99
Sparse Core Ops, SparseCore 0:
  46.6 39.0 all-gather.1
  101.7 44.1 reduce-scatter.1

commit v8 on v7

--- a/solution.py
+++ b/solution.py
@@ -97,13 +97,13 @@
     reduced_parts = lax.psum_scatter(partials, "dp", scatter_dimension=0, tiled=True)
     reduced_parts = reduced_parts.reshape(expert_count, capacity, model_width)
     reduced = lax.all_to_all(reduced_parts, "expert", split_axis=0, concat_axis=0, tiled=True)
-    reduced = reduced.astype(jnp.float32)
-    reduced = reduced.reshape(experts, capacity, model_width) + down_bias[:, None, :]
-    returned = reduced.astype(jnp.bfloat16)
-    picked = (
-        returned[columns, slots].astype(jnp.float32)
-    )
-    return jnp.sum(weights[:, :, None] * picked, axis=1).astype(jnp.bfloat16)
+    reduced = reduced.reshape(experts, capacity, model_width)
+    mixed = jnp.zeros((tok_dev, model_width), jnp.float32)
+    for k in range(TOPK):
+        row = reduced[columns[:, k], slots[:, k]].astype(jnp.float32) + down_bias[columns[:, k]]
+        row = row.astype(jnp.bfloat16).astype(jnp.float32)
+        mixed = mixed + weights[:, k : k + 1] * row
+    return mixed.astype(jnp.bfloat16)
 
 
 def solution(mesh):

time: 191 us -> 194 us (1.016)
  local copies, waits for them, and re-layouts: 7.47 us -> 15.7 us
  waiting for transfers between devices: 103 us -> 95.7 us
    gather x1 -> x8, local copies, waits for them, and re-layouts: 1.8 us -> 10.1 us  [the longest x4 5.32 us: body(): reduced[columns[:, k], slots[:, k]].astype(jnp.float32)]
    all_to_all x1, waiting for transfers between devices: 20.1 us -> 12.3 us  [body(): lax.all_to_all(reduced_parts, 'expert', split_axis=0, concat_axis=0, tile...]
  transfers between devices with their start and end apart: 3 -> 3, of which waited for: 3 -> 3; matrix products, arithmetic and copies ran while one was open for 0% -> 4% of each run, Pallas kernels for 0% -> 0%
where the time goes in v8:
time: 194 us
  waiting for transfers between devices  95.7 us (49%)
  blocking collectives  33.6 us (17%)
  matrix products  18.4 us (9%)
  local copies, waits for them, and re-layouts  15.7 us (8%)
  between operations  13.5 us (7%)
  starting transfers between devices  10.2 us (5%)
  other arithmetic  6.47 us (3%)
    reduce_scatter x1, waiting for transfers between devices, body(): lax.psum_scatter(partials, 'dp', scatter_dimension=0, tiled=True)  44.3 us
    all_gather x1, waiting for transfers between devices, body(): flat_rows = lax.all_gather(row_block, 'dp', axis=0, tiled=True)  39.1 us
    all_to_all x1, blocking collectives, body(): lax.all_to_all(outgoing, 'expert', split_axis=0, concat_axis=0, tiled=True)  33.6 us
    all_to_all x1, waiting for transfers between devices, body(): lax.all_to_all(reduced_parts, 'expert', split_axis=0, concat_axis=0, tile...  12.3 us
    all_to_all x1, starting transfers between devices, body(): lax.all_to_all(reduced_parts, 'expert', split_axis=0, concat_axis=0, tile...  10.2 us
    dot_general x1, matrix products, body(): jnp.dot(flat_rows, gate_weight, preferred_element_type=jnp.float32)  5.98 us
    dot_general x1, matrix products, body(): jnp.einsum('grf,fo->gro', hidden, down_weight, preferred_element_type=jnp...  5.42 us
    gather x4, local copies, waits for them, and re-layouts, body(): reduced[columns[:, k], slots[:, k]].astype(jnp.float32)  5.32 us
  transfers between devices with their start and end apart: 3, of which 3 were waited for; matrix products, arithmetic and copies ran while one was open for 4% of the time, Pallas kernels for 0%

profile of v8, /device:TPU:8, one launch (start us, length us, event | category | flops | bytes accessed | tf_op | source)
XLA Modules:
  0.0 193.6 jit_solution(12699287203420572481)
XLA Ops:
  6.5 0.0 copy-start
  6.5 0.0 all-gather.2.cloned.1.call-start
  6.5 1.1 select_reduce_fusion.1
  7.6 0.1 copy.15
  7.7 0.1 eq.23
  7.8 0.1 fusion.17
  7.9 0.1 reduce_window_sum.11
  8.0 0.2 select_reduce_fusion
  8.1 0.1 reshape.43
  8.2 0.1 copy.16
  8.3 0.1 convert_reduce_fusion
  8.4 1.0 fusion.14
  9.5 1.3 convolution_convert_fusion.1
  10.8 0.0 copy-done.8
  10.8 1.0 reshape.44
  11.8 33.6 %all_to_all.10 = bf16[32,4,2880]{2,1,0:T(4,128)(2,1)S(1)} all-to-all(bf16[32,4,2880]{2,1,0:T(4,128)(2,1)} %reshape.44), channel_id=1, replica_groups=mesh['dp'=8,'expert'=32] {'expert'}, dimensions={0} | all-to-all | bytes 1474560 | tf_op jit(solution)/shard_map/all_to_all | solution.py:86
  45.4 1.2 reshape.45
  46.6 0.0 all-gather.2.cloned.1.call-update
  46.7 0.0 reduce-scatter.2.cloned.1.call-start
  46.7 0.0 copy-done.6
  46.7 39.1 %all-gather.2.cloned.1.call-done = bf16[1024,2880]{1,0:T(8,128)(2,1)} async-done(((bf16[128,2880]{1,0:T(8,128)(2,1)}), bf16[1024,2880]{1,0:T(8,128)(2,1)}) %all-gather.2.cloned.1.call-update) | async-done | bytes 5898256 | tf_op jit(solution)/shard_map/all_gather | solution.py:88
  85.8 6.0 %fusion.1 = f32[1024,360]{0,1:T(8,128)S(1)} fusion(bf16[1024,2880]{1,0:T(8,128)(2,1)} %all-gather.2.cloned.1.call-done, bf16[1,2,2880,360]{2,3,1,0:T(8,128)(2,1)} %param.16), kind=kOutput, calls=%fused_computation.11 | convolution fusion | flops 2123366400 | bytes 9623552 | tf_op jit(solution)/shard_map/dot_general | solution.py:89
  91.8 0.0 copy-done.9
  91.8 4.4 %fusion.9 = bf16[45,8,8,128]{3,2,1,0:T(8,128)(2,1)S(1)} fusion(f32[1024,360]{0,1:T(8,128)S(1)} %fusion.1, bf16[1024,2880]{1,0:T(8,128)(2,1)S(1)} %copy-done.9, bf16[1,2,2880,360]{2,3,1,0:T(8,128)(2,1)} %param.16, f32[360]{0:T(512)S(1)} %get-tuple-element.6, f32[360]{0:T(512)S(1)} %get-tuple-element.5), kind=kOutput, calls=%fused_computation.18 | convolution fusion | flops 2127790080 | bytes 10232640 | tf_op jit(solution)/shard_map/dot_general | solution.py:90
  96.3 5.4 %convolution_convert_fusion = bf16[8,128,2880]{2,1,0:T(8,128)(2,1)} fusion(bf16[1,360,2880]{2,1,0:T(8,128)(2,1)S(1)} %copy-done, bf16[45,8,8,128]{3,2,1,0:T(8,128)(2,1)S(1)} %fusion.9), kind=kOutput, calls=%fused_computation.8 | convolution fusion | flops 2126315520 | bytes 8709120 | tf_op jit(solution)/shard_map/grf,fo->gro/dot_general | solution.py:93
  101.7 0.0 reduce-scatter.2.cloned.1.call-update
  101.8 0.0 copy-start.1
  101.8 44.3 %reduce-scatter.2.cloned.1.call-done = bf16[128,2880]{1,0:T(8,128)(2,1)} async-done(((bf16[1024,2880]{1,0:T(8,128)(2,1)}), bf16[128,2880]{1,0:T(8,128)(2,1)}) %reduce-scatter.2.cloned.1.call-update) | async-done | bytes 737296 | tf_op jit(solution)/shard_map/reduce_scatter | solution.py:97
  146.1 2.4 %reshape.48 = bf16[32,4,2880]{2,1,0:T(4,128)(2,1)} reshape(bf16[128,2880]{1,0:T(8,128)(2,1)} %reduce-scatter.2.cloned.1.call-done) | data formatting | bytes 1474560 | tf_op jit(solution)/shard_map/reshape | solution.py:98
  148.4 10.2 %all-to-all-start.1 = ((bf16[32,4,2880]{2,1,0:T(4,128)(2,1)}), bf16[32,4,2880]{2,1,0:T(4,128)(2,1)S(1)}, u32[]{:S(2)}, u32[]{:S(2)}) async-start(bf16[32,4,2880]{2,1,0:T(4,128)(2,1)} %reshape.48), calls=%async_computation.2 | async-start | bytes 1507328 | tf_op jit(solution)/shard_map/all_to_all | solution.py:99
  158.6 0.6 fusion.33
  159.2 0.0 copy-done.1
  159.2 0.6 gather_fusion.5
  159.8 1.3 gather_fusion.7
  161.1 1.3 pad_clamp_fusion.2
  162.4 1.4 gather_fusion.1
  163.8 1.4 gather_fusion.3
  165.2 1.2 convolution_add_fusion
  166.4 0.0 copy-done.5
  166.5 0.2 select_reduce_fusion.2
  166.7 0.6 slice_bitcast_fusion.3
  167.3 12.3 %all-to-all-done.1 = bf16[32,4,2880]{2,1,0:T(4,128)(2,1)S(1)} async-done(((bf16[32,4,2880]{2,1,0:T(4,128)(2,1)}), bf16[32,4,2880]{2,1,0:T(4,128)(2,1)S(1)}, u32[]{:S(2)}, u32[]{:S(2)}) %all-to-all-start.1) | async-done | bytes 737312 | tf_op jit(solution)/shard_map/all_to_all | solution.py:99
  179.5 0.9 gather_fusion.2
  180.4 1.5 gather_fusion.4
  181.9 1.5 gather_fusion.6
  183.4 1.5 gather_fusion
  184.9 0.0 copy-done.3
  184.9 1.9 add_convert_fusion
  (18 shorter events, 0.1 us)
Async XLA Ops:
  6.5 89.8 %copy-start = (bf16[1,360,2880]{2,1,0:T(8,128)(2,1)S(1)}, bf16[1,360,2880]{2,1,0:T(8,128)(2,1)}, u32[]{:S(2)}) copy-start(bf16[1,360,2880]{2,1,0:T(8,128)(2,1)} %param.18) | copy-start | bytes 6220804
  6.5 79.3 %all-gather.2.cloned.1.call-start = ((), (), s32[]{:S(2)}) async-start(), calls=%async_computation.3 | async-start | bytes 6782976 | tf_op jit(solution)/shard_map/all_gather | solution.py:88
  9.5 1.3 copy-start.8
  11.8 34.9 %copy-start.6 = (f32[1,2,360]{2,1,0:T(2,128)S(1)}, f32[1,2,360]{2,1,0:T(2,128)}, u32[]{:S(2)}) copy-start(f32[1,2,360]{2,1,0:T(2,128)} %param.17) | copy-start | bytes 8644
  46.7 99.4 %reduce-scatter.2.cloned.1.call-start = ((), (), s32[]{:S(2)}) async-start(), calls=%async_computation.4 | async-start | bytes 6782976 | tf_op jit(solution)/shard_map/reduce_scatter | solution.py:97
  85.8 6.0 %copy-start.9 = (bf16[1024,2880]{1,0:T(8,128)(2,1)S(1)}, bf16[1024,2880]{1,0:T(8,128)(2,1)}, u32[]{:S(2)}) copy-start(bf16[1024,2880]{1,0:T(8,128)(2,1)} %all-gather.2.cloned.1.call-done) | copy-start | bytes 17694724
  101.8 57.4 %copy-start.1 = (f32[32,2880]{1,0:T(8,128)S(1)}, f32[32,2880]{1,0:T(8,128)}, u32[]{:S(2)}) copy-start(f32[32,2880]{1,0:T(8,128)} %param.19) | copy-start | bytes 1105924
  148.4 31.1 %all-to-all-start.1 = ((bf16[32,4,2880]{2,1,0:T(4,128)(2,1)}), bf16[32,4,2880]{2,1,0:T(4,128)(2,1)S(1)}, u32[]{:S(2)}, u32[]{:S(2)}) async-start(bf16[32,4,2880]{2,1,0:T(4,128)(2,1)} %reshape.48), calls=%async_computation.2 | async-start | bytes 1507328 | tf_op jit(solution)/shard_map/all_to_all | solution.py:99
  161.1 4.1 %copy-start.4 = (bf16[16,2880]{1,0:T(8,128)(2,1)S(1)}, bf16[16,2880]{1,0:T(8,128)(2,1)}, u32[]{:S(2)}) copy-start(bf16[16,2880]{1,0:T(8,128)(2,1)} %param.10) | copy-start | bytes 276484
  161.1 5.4 %copy-start.5 = (s32[16,4]{0,1:T(4,128)S(1)}, s32[16,4]{0,1:T(4,128)}, u32[]{:S(2)}) copy-start(s32[16,4]{0,1:T(4,128)} %param.14) | copy-start | bytes 772
  165.2 19.6 %copy-start.2 = (f32[16,2880]{1,0:T(8,128)S(1)}, f32[16,2880]{1,0:T(8,128)}, u32[]{:S(2)}) copy-start(f32[16,2880]{1,0:T(8,128)} %gather_fusion.7) | copy-start | bytes 552964
  165.2 19.6 %copy-start.3 = (f32[16,2880]{1,0:T(8,128)S(1)}, f32[16,2880]{1,0:T(8,128)}, u32[]{:S(2)}) copy-start(f32[16,2880]{1,0:T(8,128)} %gather_fusion.1) | copy-start | bytes 552964
  180.4 4.5 %copy-start.7 = (f32[16]{0:T(128)S(1)}, f32[16]{0:T(128)}, u32[]{:S(2)}) copy-start(f32[16]{0:T(128)} %get-tuple-element.12) | copy-start | bytes 196
Sparse Core Ops, SparseCore 0:
  46.8 39.0 all-gather.1
  101.9 44.1 reduce-scatter.1

commit v9 on v7

--- a/solution.py
+++ b/solution.py
@@ -35,10 +35,9 @@
 
 def slot_positions(columns, experts):
     flat_ids = columns.reshape(-1)
-    expert_range = jnp.arange(experts, dtype=jnp.int32)
-    onehot = (flat_ids[:, None] == expert_range[None, :]).astype(jnp.int32)
-    before = jnp.cumsum(onehot, axis=0) - onehot
-    return jnp.sum(before * onehot, axis=1).reshape(columns.shape)
+    order = jnp.arange(flat_ids.shape[0], dtype=jnp.int32)
+    earlier = (flat_ids[:, None] == flat_ids[None, :]) & (order[None, :] < order[:, None])
+    return jnp.sum(earlier.astype(jnp.int32), axis=1).reshape(columns.shape)
 
 
 def swiglu(gate_value, up_value):

time: 191 us -> 191 us (level)
  no operation moved by 1% of the time
where the time goes in v9:
time: 191 us
  waiting for transfers between devices  103 us (54%)
  blocking collectives  33.4 us (17%)
  matrix products  17.4 us (9%)
  between operations  13.6 us (7%)
  starting transfers between devices  10.2 us (5%)
  local copies, waits for them, and re-layouts  7.47 us (4%)
  other arithmetic  5.29 us (3%)
    reduce_scatter x1, waiting for transfers between devices, body(): lax.psum_scatter(partials, 'dp', scatter_dimension=0, tiled=True)  44.2 us
    all_gather x1, waiting for transfers between devices, body(): flat_rows = lax.all_gather(row_block, 'dp', axis=0, tiled=True)  39.1 us
    all_to_all x1, blocking collectives, body(): lax.all_to_all(outgoing, 'expert', split_axis=0, concat_axis=0, tiled=True)  33.4 us
    all_to_all x1, waiting for transfers between devices, body(): lax.all_to_all(reduced_parts, 'expert', split_axis=0, concat_axis=0, tile...  20.1 us
    all_to_all x1, starting transfers between devices, body(): lax.all_to_all(reduced_parts, 'expert', split_axis=0, concat_axis=0, tile...  10.2 us
    dot_general x1, matrix products, body(): jnp.dot(flat_rows, gate_weight, preferred_element_type=jnp.float32)  5.98 us
    dot_general x1, matrix products, body(): jnp.einsum('grf,fo->gro', hidden, down_weight, preferred_element_type=jnp...  5.42 us
    dot_general x1, matrix products, body(): jnp.dot(flat_rows, up_weight, preferred_element_type=jnp.float32) + up_bias  4.45 us
  transfers between devices with their start and end apart: 3, of which 3 were waited for; matrix products, arithmetic and copies ran while one was open for 0% of the time, Pallas kernels for 0%

profile of v9, /device:TPU:8, one launch (start us, length us, event | category | flops | bytes accessed | tf_op | source)
XLA Modules:
  0.0 190.9 jit_solution(3051778041067491936)
XLA Ops:
  6.5 0.0 copy-start
  6.5 0.0 all-gather.2.cloned.1.call-start
  6.5 1.1 select_reduce_fusion
  7.6 0.1 copy.26
  7.7 0.1 eq.23
  7.8 0.2 convert_reduce_fusion.1
  8.0 0.1 reshape.106
  8.0 0.1 copy.27
  8.1 0.1 convert_reduce_fusion
  8.2 1.0 fusion.14
  9.3 1.3 convolution_convert_fusion.1
  10.6 1.0 reshape.107
  11.6 33.4 %all_to_all.10 = bf16[32,4,2880]{2,1,0:T(4,128)(2,1)S(1)} all-to-all(bf16[32,4,2880]{2,1,0:T(4,128)(2,1)} %reshape.107), channel_id=1, replica_groups=mesh['dp'=8,'expert'=32] {'expert'}, dimensions={0} | all-to-all | bytes 1474560 | tf_op jit(solution)/shard_map/all_to_all | solution.py:85
  45.1 1.2 reshape.108
  46.3 0.0 all-gather.2.cloned.1.call-update
  46.3 0.0 reduce-scatter.2.cloned.1.call-start
  46.4 0.0 copy-done.5
  46.4 39.1 %all-gather.2.cloned.1.call-done = bf16[1024,2880]{1,0:T(8,128)(2,1)} async-done(((bf16[128,2880]{1,0:T(8,128)(2,1)}), bf16[1024,2880]{1,0:T(8,128)(2,1)}) %all-gather.2.cloned.1.call-update) | async-done | bytes 5898256 | tf_op jit(solution)/shard_map/all_gather | solution.py:87
  85.5 6.0 %fusion.1 = f32[1024,360]{0,1:T(8,128)S(1)} fusion(bf16[1024,2880]{1,0:T(8,128)(2,1)} %all-gather.2.cloned.1.call-done, bf16[1,2,2880,360]{2,3,1,0:T(8,128)(2,1)} %param.16), kind=kOutput, calls=%fused_computation.4 | convolution fusion | flops 2123366400 | bytes 9623552 | tf_op jit(solution)/shard_map/dot_general | solution.py:88
  91.5 0.0 copy-done.6
  91.5 4.4 %fusion.9 = bf16[45,8,8,128]{3,2,1,0:T(8,128)(2,1)S(1)} fusion(f32[1024,360]{0,1:T(8,128)S(1)} %fusion.1, bf16[1024,2880]{1,0:T(8,128)(2,1)S(1)} %copy-done.6, bf16[1,2,2880,360]{2,3,1,0:T(8,128)(2,1)} %param.16, f32[360]{0:T(512)S(1)} %get-tuple-element.6, f32[360]{0:T(512)S(1)} %get-tuple-element.5), kind=kOutput, calls=%fused_computation.12 | convolution fusion | flops 2127790080 | bytes 10232640 | tf_op jit(solution)/shard_map/dot_general | solution.py:89
  96.0 0.0 copy-done
  96.0 5.4 %convolution_convert_fusion = bf16[8,128,2880]{2,1,0:T(8,128)(2,1)} fusion(bf16[1,360,2880]{2,1,0:T(8,128)(2,1)S(1)} %copy-done, bf16[45,8,8,128]{3,2,1,0:T(8,128)(2,1)S(1)} %fusion.9), kind=kOutput, calls=%fused_computation.1 | convolution fusion | flops 2126315520 | bytes 8709120 | tf_op jit(solution)/shard_map/grf,fo->gro/dot_general | solution.py:92
  101.4 0.0 reduce-scatter.2.cloned.1.call-update
  101.4 0.0 copy-start.2
  101.4 0.0 copy-start.3
  101.4 0.0 copy-start.7
  101.5 0.0 copy-start.8
  101.5 0.0 copy-start.4
  101.5 0.0 copy-start.1
  101.5 44.2 %reduce-scatter.2.cloned.1.call-done = bf16[128,2880]{1,0:T(8,128)(2,1)} async-done(((bf16[1024,2880]{1,0:T(8,128)(2,1)}), bf16[128,2880]{1,0:T(8,128)(2,1)}) %reduce-scatter.2.cloned.1.call-update) | async-done | bytes 737296 | tf_op jit(solution)/shard_map/reduce_scatter | solution.py:96
  145.7 2.4 %reshape.111 = bf16[32,4,2880]{2,1,0:T(4,128)(2,1)} reshape(bf16[128,2880]{1,0:T(8,128)(2,1)} %reduce-scatter.2.cloned.1.call-done) | data formatting | bytes 1474560 | tf_op jit(solution)/shard_map/reshape | solution.py:97
  148.1 10.2 %all-to-all-start.1 = ((bf16[32,4,2880]{2,1,0:T(4,128)(2,1)}), bf16[32,4,2880]{2,1,0:T(4,128)(2,1)}, u32[]{:S(2)}, u32[]{:S(2)}) async-start(bf16[32,4,2880]{2,1,0:T(4,128)(2,1)} %reshape.111), calls=%async_computation.2 | async-start | bytes 1507328 | tf_op jit(solution)/shard_map/all_to_all | solution.py:98
  158.3 0.1 reshape.112
  158.4 0.1 copy.29
  158.5 0.1 copy.32
  158.6 0.1 reshape.113
  158.7 0.0 copy-done.2
  158.7 0.0 copy-done.3
  158.7 0.0 copy-done.7
  158.7 0.2 convolution_add_fusion
  158.9 0.2 select_reduce_fusion.1
  159.1 0.1 copy.25
  159.2 20.1 %all-to-all-done.1 = bf16[32,4,2880]{2,1,0:T(4,128)(2,1)} async-done(((bf16[32,4,2880]{2,1,0:T(4,128)(2,1)}), bf16[32,4,2880]{2,1,0:T(4,128)(2,1)}, u32[]{:S(2)}, u32[]{:S(2)}) %all-to-all-start.1) | async-done | bytes 737312 | tf_op jit(solution)/shard_map/all_to_all | solution.py:98
  179.3 1.5 add_convert_fusion
  180.8 1.8 gather_fusion
  182.7 0.2 reshape.119
  182.8 1.2 multiply_reduce_fusion
  (11 shorter events, 0.1 us)
Async XLA Ops:
  6.5 89.4 %copy-start = (bf16[1,360,2880]{2,1,0:T(8,128)(2,1)S(1)}, bf16[1,360,2880]{2,1,0:T(8,128)(2,1)}, u32[]{:S(2)}) copy-start(bf16[1,360,2880]{2,1,0:T(8,128)(2,1)} %param.18) | copy-start | bytes 6220804
  6.5 79.0 %all-gather.2.cloned.1.call-start = ((), (), s32[]{:S(2)}) async-start(), calls=%async_computation.3 | async-start | bytes 6782976 | tf_op jit(solution)/shard_map/all_gather | solution.py:87
  45.1 1.3 copy-start.5
  46.3 99.4 %reduce-scatter.2.cloned.1.call-start = ((), (), s32[]{:S(2)}) async-start(), calls=%async_computation.4 | async-start | bytes 6782976 | tf_op jit(solution)/shard_map/reduce_scatter | solution.py:96
  85.5 6.0 %copy-start.6 = (bf16[1024,2880]{1,0:T(8,128)(2,1)S(1)}, bf16[1024,2880]{1,0:T(8,128)(2,1)}, u32[]{:S(2)}) copy-start(bf16[1024,2880]{1,0:T(8,128)(2,1)} %all-gather.2.cloned.1.call-done) | copy-start | bytes 17694724
  101.4 57.2 %copy-start.2 = (bf16[16,2880]{1,0:T(8,128)(2,1)S(1)}, bf16[16,2880]{1,0:T(8,128)(2,1)}, u32[]{:S(2)}) copy-start(bf16[16,2880]{1,0:T(8,128)(2,1)} %param.10) | copy-start | bytes 276484
  101.4 57.2 %copy-start.3 = (f32[2880]{0:T(1024)S(1)}, f32[2880]{0:T(1024)}, u32[]{:S(2)}) copy-start(f32[2880]{0:T(1024)} %param.11) | copy-start | bytes 34564
  101.4 57.2 %copy-start.7 = (bf16[2880,32]{0,1:T(8,128)(2,1)S(1)}, bf16[2880,32]{0,1:T(8,128)(2,1)}, u32[]{:S(2)}) copy-start(bf16[2880,32]{0,1:T(8,128)(2,1)} %param.12) | copy-start | bytes 552964
  101.5 57.2 %copy-start.8 = (f32[32]{0:T(128)S(1)}, f32[32]{0:T(128)}, u32[]{:S(2)}) copy-start(f32[32]{0:T(128)} %param.13) | copy-start | bytes 388
  101.5 57.5 %copy-start.4 = (s32[16,4]{0,1:T(4,128)S(1)}, s32[16,4]{0,1:T(4,128)}, u32[]{:S(2)}) copy-start(s32[16,4]{0,1:T(4,128)} %param.14) | copy-start | bytes 772
  101.5 77.8 %copy-start.1 = (f32[32,2880]{1,0:T(8,128)S(1)}, f32[32,2880]{1,0:T(8,128)}, u32[]{:S(2)}) copy-start(f32[32,2880]{1,0:T(8,128)} %param.19) | copy-start | bytes 1105924
  148.1 31.2 %all-to-all-start.1 = ((bf16[32,4,2880]{2,1,0:T(4,128)(2,1)}), bf16[32,4,2880]{2,1,0:T(4,128)(2,1)}, u32[]{:S(2)}, u32[]{:S(2)}) async-start(bf16[32,4,2880]{2,1,0:T(4,128)(2,1)} %reshape.111), calls=%async_computation.2 | async-start | bytes 1507328 | tf_op jit(solution)/shard_map/all_to_all | solution.py:98
Sparse Core Ops, SparseCore 0:
  46.5 39.0 all-gather.1
  101.5 44.1 reduce-scatter.1

commit v10 on v9

--- a/solution.py
+++ b/solution.py
@@ -28,9 +28,7 @@
 
 
 def lookup(expert_ids, placement):
-    expert_range = jnp.arange(placement.shape[0], dtype=jnp.int32)
-    matches = expert_ids[:, :, None] == expert_range[None, None, :]
-    return jnp.sum(jnp.where(matches, placement[None, None, :], 0), axis=2)
+    return jnp.take(placement, expert_ids, mode="clip")
 
 
 def slot_positions(columns, experts):

time: 191 us -> 190 us (level)
  other arithmetic: 5.29 us -> 3.34 us
where the time goes in v10:
time: 190 us
  waiting for transfers between devices  103 us (54%)
  blocking collectives  33.4 us (18%)
  matrix products  16.5 us (9%)
  between operations  13.6 us (7%)
  starting transfers between devices  10.4 us (5%)
  local copies, waits for them, and re-layouts  9 us (5%)
  other arithmetic  3.34 us (2%)
    reduce_scatter x1, waiting for transfers between devices, body(): lax.psum_scatter(partials, 'dp', scatter_dimension=0, tiled=True)  44.3 us
    all_gather x1, waiting for transfers between devices, body(): flat_rows = lax.all_gather(row_block, 'dp', axis=0, tiled=True)  39.1 us
    all_to_all x1, blocking collectives, body(): lax.all_to_all(outgoing, 'expert', split_axis=0, concat_axis=0, tiled=True)  33.4 us
    all_to_all x1, waiting for transfers between devices, body(): lax.all_to_all(reduced_parts, 'expert', split_axis=0, concat_axis=0, tile...  20 us
    all_to_all x1, starting transfers between devices, body(): lax.all_to_all(reduced_parts, 'expert', split_axis=0, concat_axis=0, tile...  10.4 us
    dot_general x1, matrix products, body(): jnp.dot(flat_rows, gate_weight, preferred_element_type=jnp.float32)  5.98 us
    dot_general x1, matrix products, body(): jnp.einsum('grf,fo->gro', hidden, down_weight, preferred_element_type=jnp...  5.42 us
    dot_general x1, matrix products, body(): jnp.dot(flat_rows, up_weight, preferred_element_type=jnp.float32) + up_bias  4.45 us
  transfers between devices with their start and end apart: 3, of which 3 were waited for; matrix products, arithmetic and copies ran while one was open for 0% of the time, Pallas kernels for 0%

profile of v10, /device:TPU:8, one launch (start us, length us, event | category | flops | bytes accessed | tf_op | source)
XLA Modules:
  0.0 189.7 jit_solution(691636519580747986)
XLA Ops:
  6.5 0.0 copy-start
  6.5 0.0 all-gather.2.cloned.1.call-start
  6.5 0.9 copy.18
  7.5 0.1 reshape.114
  7.6 0.0 copy-done.1
  7.6 0.0 copy-start.3
  7.6 0.0 copy-start.4
  7.6 0.8 gather_fusion
  8.4 0.2 convert_reduce_fusion.1
  8.6 0.1 reshape.133
  8.6 0.1 copy.19
  8.7 0.1 convert_reduce_fusion
  8.8 0.0 copy-done.3
  8.8 0.1 fusion.14
  9.0 0.0 copy-done.4
  9.0 0.4 convolution_convert_fusion.1
  9.4 1.0 reshape.106
  10.5 33.4 %all_to_all.10 = bf16[32,4,2880]{2,1,0:T(4,128)(2,1)S(1)} all-to-all(bf16[32,4,2880]{2,1,0:T(4,128)(2,1)} %reshape.106), channel_id=1, replica_groups=mesh['dp'=8,'expert'=32] {'expert'}, dimensions={0} | all-to-all | bytes 1474560 | tf_op jit(solution)/shard_map/all_to_all | solution.py:83
  43.9 1.2 reshape.107
  45.1 0.0 all-gather.2.cloned.1.call-update
  45.2 0.0 reduce-scatter.2.cloned.1.call-start
  45.2 0.0 copy-done.6
  45.2 39.1 %all-gather.2.cloned.1.call-done = bf16[1024,2880]{1,0:T(8,128)(2,1)} async-done(((bf16[128,2880]{1,0:T(8,128)(2,1)}), bf16[1024,2880]{1,0:T(8,128)(2,1)}) %all-gather.2.cloned.1.call-update) | async-done | bytes 5898256 | tf_op jit(solution)/shard_map/all_gather | solution.py:85
  84.3 6.0 %fusion.1 = f32[1024,360]{0,1:T(8,128)S(1)} fusion(bf16[1024,2880]{1,0:T(8,128)(2,1)} %all-gather.2.cloned.1.call-done, bf16[1,2,2880,360]{2,3,1,0:T(8,128)(2,1)} %param.16), kind=kOutput, calls=%fused_computation.5 | convolution fusion | flops 2123366400 | bytes 9623552 | tf_op jit(solution)/shard_map/dot_general | solution.py:86
  90.3 0.0 copy-done.7
  90.3 4.4 %fusion.9 = bf16[45,8,8,128]{3,2,1,0:T(8,128)(2,1)S(1)} fusion(f32[1024,360]{0,1:T(8,128)S(1)} %fusion.1, bf16[1024,2880]{1,0:T(8,128)(2,1)S(1)} %copy-done.7, bf16[1,2,2880,360]{2,3,1,0:T(8,128)(2,1)} %param.16, f32[360]{0:T(512)S(1)} %get-tuple-element.6, f32[360]{0:T(512)S(1)} %get-tuple-element.5), kind=kOutput, calls=%fused_computation.13 | convolution fusion | flops 2127790080 | bytes 10232640 | tf_op jit(solution)/shard_map/dot_general | solution.py:87
  94.8 5.4 %convolution_convert_fusion = bf16[8,128,2880]{2,1,0:T(8,128)(2,1)} fusion(bf16[1,360,2880]{2,1,0:T(8,128)(2,1)S(1)} %copy-done, bf16[45,8,8,128]{3,2,1,0:T(8,128)(2,1)S(1)} %fusion.9), kind=kOutput, calls=%fused_computation.2 | convolution fusion | flops 2126315520 | bytes 8709120 | tf_op jit(solution)/shard_map/grf,fo->gro/dot_general | solution.py:90
  100.2 0.0 reduce-scatter.2.cloned.1.call-update
  100.2 0.0 copy-start.8
  100.3 0.0 copy-start.9
  100.3 0.0 copy-start.5
  100.3 0.0 copy-start.2
  100.3 44.3 %reduce-scatter.2.cloned.1.call-done = bf16[128,2880]{1,0:T(8,128)(2,1)} async-done(((bf16[1024,2880]{1,0:T(8,128)(2,1)}), bf16[128,2880]{1,0:T(8,128)(2,1)}) %reduce-scatter.2.cloned.1.call-update) | async-done | bytes 737296 | tf_op jit(solution)/shard_map/reduce_scatter | solution.py:94
  144.5 2.4 %reshape.110 = bf16[32,4,2880]{2,1,0:T(4,128)(2,1)} reshape(bf16[128,2880]{1,0:T(8,128)(2,1)} %reduce-scatter.2.cloned.1.call-done) | data formatting | bytes 1474560 | tf_op jit(solution)/shard_map/reshape | solution.py:95
  146.9 10.4 %all-to-all-start.1 = ((bf16[32,4,2880]{2,1,0:T(4,128)(2,1)}), bf16[32,4,2880]{2,1,0:T(4,128)(2,1)}, u32[]{:S(2)}, u32[]{:S(2)}) async-start(bf16[32,4,2880]{2,1,0:T(4,128)(2,1)} %reshape.110), calls=%async_computation.2 | async-start | bytes 1507328 | tf_op jit(solution)/shard_map/all_to_all | solution.py:96
  157.3 0.1 reshape.111
  157.4 0.1 gather.10
  157.5 0.1 reshape.120
  157.6 0.0 copy-done.8
  157.6 0.0 copy-done.9
  157.6 0.2 convolution_add_fusion
  157.8 0.2 select_reduce_fusion
  158.0 0.1 copy.17
  158.1 20.0 %all-to-all-done.1 = bf16[32,4,2880]{2,1,0:T(4,128)(2,1)} async-done(((bf16[32,4,2880]{2,1,0:T(4,128)(2,1)}), bf16[32,4,2880]{2,1,0:T(4,128)(2,1)}, u32[]{:S(2)}, u32[]{:S(2)}) %all-to-all-start.1) | async-done | bytes 737312 | tf_op jit(solution)/shard_map/all_to_all | solution.py:96
  178.1 1.5 add_convert_fusion
  179.7 1.8 gather_fusion.1
  181.5 0.2 reshape.132
  181.7 1.2 multiply_reduce_fusion
  (13 shorter events, 0.1 us)
Async XLA Ops:
  6.5 88.3 %copy-start = (bf16[1,360,2880]{2,1,0:T(8,128)(2,1)S(1)}, bf16[1,360,2880]{2,1,0:T(8,128)(2,1)}, u32[]{:S(2)}) copy-start(bf16[1,360,2880]{2,1,0:T(8,128)(2,1)} %param.18) | copy-start | bytes 6220804
  6.5 1.0 copy-start.1
  6.5 77.8 %all-gather.2.cloned.1.call-start = ((), (), s32[]{:S(2)}) async-start(), calls=%async_computation.3 | async-start | bytes 6782976 | tf_op jit(solution)/shard_map/all_gather | solution.py:85
  7.6 1.3 copy-start.3
  7.6 1.4 copy-start.4
  43.9 1.3 copy-start.6
  45.2 99.4 %reduce-scatter.2.cloned.1.call-start = ((), (), s32[]{:S(2)}) async-start(), calls=%async_computation.4 | async-start | bytes 6782976 | tf_op jit(solution)/shard_map/reduce_scatter | solution.py:94
  84.3 6.0 %copy-start.7 = (bf16[1024,2880]{1,0:T(8,128)(2,1)S(1)}, bf16[1024,2880]{1,0:T(8,128)(2,1)}, u32[]{:S(2)}) copy-start(bf16[1024,2880]{1,0:T(8,128)(2,1)} %all-gather.2.cloned.1.call-done) | copy-start | bytes 17694724
  100.2 57.3 %copy-start.8 = (bf16[2880,32]{0,1:T(8,128)(2,1)S(1)}, bf16[2880,32]{0,1:T(8,128)(2,1)}, u32[]{:S(2)}) copy-start(bf16[2880,32]{0,1:T(8,128)(2,1)} %param.12) | copy-start | bytes 552964
  100.3 57.3 %copy-start.9 = (f32[32]{0:T(128)S(1)}, f32[32]{0:T(128)}, u32[]{:S(2)}) copy-start(f32[32]{0:T(128)} %param.13) | copy-start | bytes 388
  100.3 57.6 %copy-start.5 = (s32[16,4]{0,1:T(4,128)S(1)}, s32[16,4]{0,1:T(4,128)}, u32[]{:S(2)}) copy-start(s32[16,4]{0,1:T(4,128)} %param.14) | copy-start | bytes 772
  100.3 77.9 %copy-start.2 = (f32[32,2880]{1,0:T(8,128)S(1)}, f32[32,2880]{1,0:T(8,128)}, u32[]{:S(2)}) copy-start(f32[32,2880]{1,0:T(8,128)} %param.19) | copy-start | bytes 1105924
  146.9 31.2 %all-to-all-start.1 = ((bf16[32,4,2880]{2,1,0:T(4,128)(2,1)}), bf16[32,4,2880]{2,1,0:T(4,128)(2,1)}, u32[]{:S(2)}, u32[]{:S(2)}) async-start(bf16[32,4,2880]{2,1,0:T(4,128)(2,1)} %reshape.110), calls=%async_computation.2 | async-start | bytes 1507328 | tf_op jit(solution)/shard_map/all_to_all | solution.py:96
Sparse Core Ops, SparseCore 0:
  45.3 38.9 all-gather.1
  100.4 44.1 reduce-scatter.1

commit v11 on v10

--- a/solution.py
+++ b/solution.py
@@ -94,13 +94,10 @@
     reduced_parts = lax.psum_scatter(partials, "dp", scatter_dimension=0, tiled=True)
     reduced_parts = reduced_parts.reshape(expert_count, capacity, model_width)
     reduced = lax.all_to_all(reduced_parts, "expert", split_axis=0, concat_axis=0, tiled=True)
-    reduced = reduced.astype(jnp.float32)
-    reduced = reduced.reshape(experts, capacity, model_width) + down_bias[:, None, :]
-    returned = reduced.astype(jnp.bfloat16)
-    picked = (
-        returned[columns, slots].astype(jnp.float32)
-    )
-    return jnp.sum(weights[:, :, None] * picked, axis=1).astype(jnp.bfloat16)
+    reduced = reduced.reshape(experts, capacity, model_width)
+    picked = reduced[columns.T, slots.T].astype(jnp.float32) + down_bias[columns.T]
+    picked = picked.astype(jnp.bfloat16).astype(jnp.float32)
+    return jnp.sum(weights.T[:, :, None] * picked, axis=0).astype(jnp.bfloat16)
 
 
 def solution(mesh):

time: 190 us -> 189 us (level)
  waiting for transfers between devices: 103 us -> 101 us
    all_to_all x1, waiting for transfers between devices: 20 us -> 17.3 us  [body(): lax.all_to_all(reduced_parts, 'expert', split_axis=0, concat_axis=0, tile...]
  transfers between devices with their start and end apart: 3 -> 3, of which waited for: 3 -> 3; matrix products, arithmetic and copies ran while one was open for 0% -> 2% of each run, Pallas kernels for 0% -> 0%
where the time goes in v11:
time: 189 us
  waiting for transfers between devices  101 us (53%)
  blocking collectives  33.6 us (18%)
  matrix products  17.4 us (9%)
  between operations  13.6 us (7%)
  local copies, waits for them, and re-layouts  10.6 us (6%)
  starting transfers between devices  10.4 us (6%)
  other arithmetic  2.61 us (1%)
    reduce_scatter x1, waiting for transfers between devices, body(): lax.psum_scatter(partials, 'dp', scatter_dimension=0, tiled=True)  44.3 us
    all_gather x1, waiting for transfers between devices, body(): flat_rows = lax.all_gather(row_block, 'dp', axis=0, tiled=True)  39.1 us
    all_to_all x1, blocking collectives, body(): lax.all_to_all(outgoing, 'expert', split_axis=0, concat_axis=0, tiled=True)  33.6 us
    all_to_all x1, waiting for transfers between devices, body(): lax.all_to_all(reduced_parts, 'expert', split_axis=0, concat_axis=0, tile...  17.3 us
    all_to_all x1, starting transfers between devices, body(): lax.all_to_all(reduced_parts, 'expert', split_axis=0, concat_axis=0, tile...  10.3 us
    dot_general x1, matrix products, body(): jnp.dot(flat_rows, gate_weight, preferred_element_type=jnp.float32)  5.98 us
    dot_general x1, matrix products, body(): jnp.einsum('grf,fo->gro', hidden, down_weight, preferred_element_type=jnp...  5.42 us
    dot_general x1, matrix products, body(): jnp.dot(flat_rows, up_weight, preferred_element_type=jnp.float32) + up_bias  4.45 us
  transfers between devices with their start and end apart: 3, of which 3 were waited for; matrix products, arithmetic and copies ran while one was open for 2% of the time, Pallas kernels for 0%

profile of v11, /device:TPU:8, one launch (start us, length us, event | category | flops | bytes accessed | tf_op | source)
XLA Modules:
  0.0 188.9 jit_solution(12569673349516595402)
XLA Ops:
  6.5 0.0 copy-start
  6.5 0.0 all-gather.2.cloned.1.call-start
  6.5 0.9 copy.21
  7.5 0.1 reshape.52
  7.6 0.0 copy-done.1
  7.6 0.0 copy-start.3
  7.6 0.0 copy-start.4
  7.6 0.8 gather_fusion
  8.4 0.2 convert_reduce_fusion.1
  8.6 0.1 reshape.51
  8.6 0.1 reshape.44
  8.7 0.1 copy.22
  8.8 0.1 convert_reduce_fusion
  8.9 0.0 copy-done.3
  8.9 0.1 fusion.15
  9.1 0.0 copy-done.4
  9.1 0.4 convolution_convert_fusion.1
  9.5 1.0 reshape.45
  10.5 33.6 %all_to_all.10 = bf16[32,4,2880]{2,1,0:T(4,128)(2,1)S(1)} all-to-all(bf16[32,4,2880]{2,1,0:T(4,128)(2,1)} %reshape.45), channel_id=1, replica_groups=mesh['dp'=8,'expert'=32] {'expert'}, dimensions={0} | all-to-all | bytes 1474560 | tf_op jit(solution)/shard_map/all_to_all | solution.py:83
  44.1 1.2 reshape.46
  45.4 0.0 all-gather.2.cloned.1.call-update
  45.4 0.0 reduce-scatter.2.cloned.1.call-start
  45.4 0.0 copy-done.6
  45.5 39.1 %all-gather.2.cloned.1.call-done = bf16[1024,2880]{1,0:T(8,128)(2,1)} async-done(((bf16[128,2880]{1,0:T(8,128)(2,1)}), bf16[1024,2880]{1,0:T(8,128)(2,1)}) %all-gather.2.cloned.1.call-update) | async-done | bytes 5898256 | tf_op jit(solution)/shard_map/all_gather | solution.py:85
  84.6 6.0 %fusion.1 = f32[1024,360]{0,1:T(8,128)S(1)} fusion(bf16[1024,2880]{1,0:T(8,128)(2,1)} %all-gather.2.cloned.1.call-done, bf16[1,2,2880,360]{2,3,1,0:T(8,128)(2,1)} %param.16), kind=kOutput, calls=%fused_computation.6 | convolution fusion | flops 2123366400 | bytes 9623552 | tf_op jit(solution)/shard_map/dot_general | solution.py:86
  90.5 0.0 copy-done.7
  90.5 4.4 %fusion.9 = bf16[45,8,8,128]{3,2,1,0:T(8,128)(2,1)S(1)} fusion(f32[1024,360]{0,1:T(8,128)S(1)} %fusion.1, bf16[1024,2880]{1,0:T(8,128)(2,1)S(1)} %copy-done.7, bf16[1,2,2880,360]{2,3,1,0:T(8,128)(2,1)} %param.16, f32[360]{0:T(512)S(1)} %get-tuple-element.6, f32[360]{0:T(512)S(1)} %get-tuple-element.5), kind=kOutput, calls=%fused_computation.13 | convolution fusion | flops 2127790080 | bytes 10232640 | tf_op jit(solution)/shard_map/dot_general | solution.py:87
  95.0 0.0 copy-done
  95.0 5.4 %convolution_convert_fusion = bf16[8,128,2880]{2,1,0:T(8,128)(2,1)} fusion(bf16[1,360,2880]{2,1,0:T(8,128)(2,1)S(1)} %copy-done, bf16[45,8,8,128]{3,2,1,0:T(8,128)(2,1)S(1)} %fusion.9), kind=kOutput, calls=%fused_computation.3 | convolution fusion | flops 2126315520 | bytes 8709120 | tf_op jit(solution)/shard_map/grf,fo->gro/dot_general | solution.py:90
  100.4 0.0 reduce-scatter.2.cloned.1.call-update
  100.5 0.0 copy-start.2
  100.5 44.3 %reduce-scatter.2.cloned.1.call-done = bf16[128,2880]{1,0:T(8,128)(2,1)} async-done(((bf16[1024,2880]{1,0:T(8,128)(2,1)}), bf16[128,2880]{1,0:T(8,128)(2,1)}) %reduce-scatter.2.cloned.1.call-update) | async-done | bytes 737296 | tf_op jit(solution)/shard_map/reduce_scatter | solution.py:94
  144.8 2.4 %reshape.49 = bf16[32,4,2880]{2,1,0:T(4,128)(2,1)} reshape(bf16[128,2880]{1,0:T(8,128)(2,1)} %reduce-scatter.2.cloned.1.call-done) | data formatting | bytes 1474560 | tf_op jit(solution)/shard_map/reshape | solution.py:95
  147.1 10.3 %all-to-all-start.1 = ((bf16[32,4,2880]{2,1,0:T(4,128)(2,1)}), bf16[32,4,2880]{2,1,0:T(4,128)(2,1)S(1)}, u32[]{:S(2)}, u32[]{:S(2)}) async-start(bf16[32,4,2880]{2,1,0:T(4,128)(2,1)} %reshape.49), calls=%async_computation.2 | async-start | bytes 1507328 | tf_op jit(solution)/shard_map/all_to_all | solution.py:96
  157.5 0.1 copy.24
  157.6 0.1 reshape.58
  157.6 0.1 copy.25
  157.7 0.1 reshape.66
  157.8 0.0 copy-start.8
  157.8 0.0 copy-start.5
  157.9 1.7 gather_fusion.2
  159.6 1.1 convolution_add_fusion
  160.7 0.0 copy-done.5
  160.7 0.2 select_reduce_fusion
  160.9 17.3 %all-to-all-done.1 = bf16[32,4,2880]{2,1,0:T(4,128)(2,1)S(1)} async-done(((bf16[32,4,2880]{2,1,0:T(4,128)(2,1)}), bf16[32,4,2880]{2,1,0:T(4,128)(2,1)S(1)}, u32[]{:S(2)}, u32[]{:S(2)}) %all-to-all-start.1) | async-done | bytes 737312 | tf_op jit(solution)/shard_map/all_to_all | solution.py:96
  178.2 1.8 gather_fusion.1
  180.1 1.2 add_convert_fusion
  181.3 0.8 fusion.12
  (13 shorter events, 0.1 us)
Async XLA Ops:
  6.5 88.5 %copy-start = (bf16[1,360,2880]{2,1,0:T(8,128)(2,1)S(1)}, bf16[1,360,2880]{2,1,0:T(8,128)(2,1)}, u32[]{:S(2)}) copy-start(bf16[1,360,2880]{2,1,0:T(8,128)(2,1)} %param.18) | copy-start | bytes 6220804
  6.5 1.0 copy-start.1
  6.5 78.0 %all-gather.2.cloned.1.call-start = ((), (), s32[]{:S(2)}) async-start(), calls=%async_computation.3 | async-start | bytes 6782976 | tf_op jit(solution)/shard_map/all_gather | solution.py:85
  7.6 1.3 copy-start.3
  7.6 1.5 copy-start.4
  10.5 34.9 %copy-start.6 = (f32[1,2,360]{2,1,0:T(2,128)S(1)}, f32[1,2,360]{2,1,0:T(2,128)}, u32[]{:S(2)}) copy-start(f32[1,2,360]{2,1,0:T(2,128)} %param.17) | copy-start | bytes 8644
  45.4 99.4 %reduce-scatter.2.cloned.1.call-start = ((), (), s32[]{:S(2)}) async-start(), calls=%async_computation.4 | async-start | bytes 6782976 | tf_op jit(solution)/shard_map/reduce_scatter | solution.py:94
  84.5 6.0 %copy-start.7 = (bf16[1024,2880]{1,0:T(8,128)(2,1)S(1)}, bf16[1024,2880]{1,0:T(8,128)(2,1)}, u32[]{:S(2)}) copy-start(bf16[1024,2880]{1,0:T(8,128)(2,1)} %all-gather.2.cloned.1.call-done) | copy-start | bytes 17694724
  100.5 57.4 %copy-start.2 = (f32[32,2880]{1,0:T(8,128)S(1)}, f32[32,2880]{1,0:T(8,128)}, u32[]{:S(2)}) copy-start(f32[32,2880]{1,0:T(8,128)} %param.19) | copy-start | bytes 1105924
  147.1 31.1 %all-to-all-start.1 = ((bf16[32,4,2880]{2,1,0:T(4,128)(2,1)}), bf16[32,4,2880]{2,1,0:T(4,128)(2,1)S(1)}, u32[]{:S(2)}, u32[]{:S(2)}) async-start(bf16[32,4,2880]{2,1,0:T(4,128)(2,1)} %reshape.49), calls=%async_computation.2 | async-start | bytes 1507328 | tf_op jit(solution)/shard_map/all_to_all | solution.py:96
  157.8 1.7 copy-start.8
  157.8 2.9 %copy-start.5 = (s32[16,4]{0,1:T(4,128)S(1)}, s32[16,4]{0,1:T(4,128)}, u32[]{:S(2)}) copy-start(s32[16,4]{0,1:T(4,128)} %param.14) | copy-start | bytes 772
Sparse Core Ops, SparseCore 0:
  45.5 39.0 all-gather.1
  100.6 44.1 reduce-scatter.1

commit v12 on v11

--- a/solution.py
+++ b/solution.py
@@ -65,11 +65,12 @@
     normed = normalize(tokens, norm_gain)
     weights = routing(normed, router_weight, router_bias, expert_ids)
     columns = lookup(expert_ids, placement)
+    columns = columns.T
     slots = slot_positions(columns, experts)
     target_row = columns * capacity + slots
     targets = jnp.arange(experts * capacity, dtype=jnp.int32)
     dispatch = jnp.sum(
-        (target_row[:, :, None] == targets[None, None, :]).astype(jnp.int32), axis=1
+        (target_row[:, :, None] == targets[None, None, :]).astype(jnp.int32), axis=0
     ).astype(jnp.bfloat16)
     outgoing = jnp.dot(dispatch.T, normed, preferred_element_type=jnp.float32).astype(jnp.bfloat16)
     outgoing = with_layout_constraint(outgoing, Layout(major_to_minor=(0, 1)))
@@ -95,7 +96,7 @@
     reduced_parts = reduced_parts.reshape(expert_count, capacity, model_width)
     reduced = lax.all_to_all(reduced_parts, "expert", split_axis=0, concat_axis=0, tiled=True)
     reduced = reduced.reshape(experts, capacity, model_width)
-    picked = reduced[columns.T, slots.T].astype(jnp.float32) + down_bias[columns.T]
+    picked = reduced[columns, slots].astype(jnp.float32) + down_bias[columns]
     picked = picked.astype(jnp.bfloat16).astype(jnp.float32)
     return jnp.sum(weights.T[:, :, None] * picked, axis=0).astype(jnp.bfloat16)
 

time: 189 us -> 189 us (level)
  no operation moved by 1% of the time
where the time goes in v12:
time: 189 us
  waiting for transfers between devices  101 us (53%)
  blocking collectives  33.6 us (18%)
  matrix products  17.4 us (9%)
  between operations  13.6 us (7%)
  local copies, waits for them, and re-layouts  10.6 us (6%)
  starting transfers between devices  10.2 us (5%)
  other arithmetic  2.62 us (1%)
    reduce_scatter x1, waiting for transfers between devices, body(): lax.psum_scatter(partials, 'dp', scatter_dimension=0, tiled=True)  44.7 us
    all_gather x1, waiting for transfers between devices, body(): flat_rows = lax.all_gather(row_block, 'dp', axis=0, tiled=True)  39.1 us
    all_to_all x1, blocking collectives, body(): lax.all_to_all(outgoing, 'expert', split_axis=0, concat_axis=0, tiled=True)  33.6 us
    all_to_all x1, waiting for transfers between devices, body(): lax.all_to_all(reduced_parts, 'expert', split_axis=0, concat_axis=0, tile...  17.1 us
    all_to_all x1, starting transfers between devices, body(): lax.all_to_all(reduced_parts, 'expert', split_axis=0, concat_axis=0, tile...  10.2 us
    dot_general x1, matrix products, body(): jnp.dot(flat_rows, gate_weight, preferred_element_type=jnp.float32)  5.98 us
    dot_general x1, matrix products, body(): jnp.einsum('grf,fo->gro', hidden, down_weight, preferred_element_type=jnp...  5.42 us
    dot_general x1, matrix products, body(): jnp.dot(flat_rows, up_weight, preferred_element_type=jnp.float32) + up_bias  4.45 us
  transfers between devices with their start and end apart: 3, of which 3 were waited for; matrix products, arithmetic and copies ran while one was open for 2% of the time, Pallas kernels for 0%

profile of v12, /device:TPU:8, one launch (start us, length us, event | category | flops | bytes accessed | tf_op | source)
XLA Modules:
  0.0 189.0 jit_solution(2817845586696166762)
XLA Ops:
  6.5 0.0 copy-start
  6.5 0.0 all-gather.2.cloned.1.call-start
  6.5 0.9 copy.34
  7.5 0.1 reshape.76
  7.6 0.0 copy-done.1
  7.6 0.0 copy-start.3
  7.6 0.0 copy-start.4
  7.6 0.8 gather_fusion
  8.4 0.1 reshape.75
  8.5 0.1 copy.35
  8.5 0.1 eq.44
  8.6 0.2 convert_reduce_fusion.1
  8.8 0.1 reshape.67
  8.9 0.1 convert_reduce_fusion
  9.0 0.0 copy-done.3
  9.0 0.1 fusion.15
  9.2 0.0 copy-done.4
  9.2 0.4 convolution_convert_fusion.1
  9.6 1.0 reshape.68
  10.6 33.6 %all_to_all.10 = bf16[32,4,2880]{2,1,0:T(4,128)(2,1)S(1)} all-to-all(bf16[32,4,2880]{2,1,0:T(4,128)(2,1)} %reshape.68), channel_id=1, replica_groups=mesh['dp'=8,'expert'=32] {'expert'}, dimensions={0} | all-to-all | bytes 1474560 | tf_op jit(solution)/shard_map/all_to_all | solution.py:84
  44.2 1.2 reshape.69
  45.4 0.0 all-gather.2.cloned.1.call-update
  45.5 0.0 reduce-scatter.2.cloned.1.call-start
  45.5 0.0 copy-done.6
  45.6 39.1 %all-gather.2.cloned.1.call-done = bf16[1024,2880]{1,0:T(8,128)(2,1)} async-done(((bf16[128,2880]{1,0:T(8,128)(2,1)}), bf16[1024,2880]{1,0:T(8,128)(2,1)}) %all-gather.2.cloned.1.call-update) | async-done | bytes 5898256 | tf_op jit(solution)/shard_map/all_gather | solution.py:86
  84.6 6.0 %fusion.1 = f32[1024,360]{0,1:T(8,128)S(1)} fusion(bf16[1024,2880]{1,0:T(8,128)(2,1)} %all-gather.2.cloned.1.call-done, bf16[1,2,2880,360]{2,3,1,0:T(8,128)(2,1)} %param.16), kind=kOutput, calls=%fused_computation.6 | convolution fusion | flops 2123366400 | bytes 9623552 | tf_op jit(solution)/shard_map/dot_general | solution.py:87
  90.6 0.0 copy-done.7
  90.6 4.5 %fusion.9 = bf16[45,8,8,128]{3,2,1,0:T(8,128)(2,1)S(1)} fusion(f32[1024,360]{0,1:T(8,128)S(1)} %fusion.1, bf16[1024,2880]{1,0:T(8,128)(2,1)S(1)} %copy-done.7, bf16[1,2,2880,360]{2,3,1,0:T(8,128)(2,1)} %param.16, f32[360]{0:T(512)S(1)} %get-tuple-element.6, f32[360]{0:T(512)S(1)} %get-tuple-element.5), kind=kOutput, calls=%fused_computation.13 | convolution fusion | flops 2127790080 | bytes 10232640 | tf_op jit(solution)/shard_map/dot_general | solution.py:88
  95.1 0.0 copy-done
  95.1 5.4 %convolution_convert_fusion = bf16[8,128,2880]{2,1,0:T(8,128)(2,1)} fusion(bf16[1,360,2880]{2,1,0:T(8,128)(2,1)S(1)} %copy-done, bf16[45,8,8,128]{3,2,1,0:T(8,128)(2,1)S(1)} %fusion.9), kind=kOutput, calls=%fused_computation.3 | convolution fusion | flops 2126315520 | bytes 8709120 | tf_op jit(solution)/shard_map/grf,fo->gro/dot_general | solution.py:91
  100.5 0.0 reduce-scatter.2.cloned.1.call-update
  100.5 0.0 copy-start.2
  100.6 44.7 %reduce-scatter.2.cloned.1.call-done = bf16[128,2880]{1,0:T(8,128)(2,1)} async-done(((bf16[1024,2880]{1,0:T(8,128)(2,1)}), bf16[128,2880]{1,0:T(8,128)(2,1)}) %reduce-scatter.2.cloned.1.call-update) | async-done | bytes 737296 | tf_op jit(solution)/shard_map/reduce_scatter | solution.py:95
  145.3 2.4 %reshape.72 = bf16[32,4,2880]{2,1,0:T(4,128)(2,1)} reshape(bf16[128,2880]{1,0:T(8,128)(2,1)} %reduce-scatter.2.cloned.1.call-done) | data formatting | bytes 1474560 | tf_op jit(solution)/shard_map/reshape | solution.py:96
  147.7 10.2 %all-to-all-start.1 = ((bf16[32,4,2880]{2,1,0:T(4,128)(2,1)}), bf16[32,4,2880]{2,1,0:T(4,128)(2,1)S(1)}, u32[]{:S(2)}, u32[]{:S(2)}) async-start(bf16[32,4,2880]{2,1,0:T(4,128)(2,1)} %reshape.72), calls=%async_computation.2 | async-start | bytes 1507328 | tf_op jit(solution)/shard_map/all_to_all | solution.py:97
  157.8 0.1 reshape.73
  157.9 0.1 reshape.82
  158.0 0.1 reshape.90
  158.1 0.0 copy-start.8
  158.1 0.0 copy-start.5
  158.1 1.7 gather_fusion.2
  159.8 1.1 convolution_add_fusion
  161.0 0.0 copy-done.5
  161.0 0.2 select_reduce_fusion
  161.2 17.1 %all-to-all-done.1 = bf16[32,4,2880]{2,1,0:T(4,128)(2,1)S(1)} async-done(((bf16[32,4,2880]{2,1,0:T(4,128)(2,1)}), bf16[32,4,2880]{2,1,0:T(4,128)(2,1)S(1)}, u32[]{:S(2)}, u32[]{:S(2)}) %all-to-all-start.1) | async-done | bytes 737312 | tf_op jit(solution)/shard_map/all_to_all | solution.py:97
  178.3 1.8 gather_fusion.1
  180.1 1.2 add_convert_fusion
  181.3 0.8 fusion.12
  (13 shorter events, 0.1 us)
Async XLA Ops:
  6.5 88.6 %copy-start = (bf16[1,360,2880]{2,1,0:T(8,128)(2,1)S(1)}, bf16[1,360,2880]{2,1,0:T(8,128)(2,1)}, u32[]{:S(2)}) copy-start(bf16[1,360,2880]{2,1,0:T(8,128)(2,1)} %param.18) | copy-start | bytes 6220804
  6.5 1.0 copy-start.1
  6.5 78.1 %all-gather.2.cloned.1.call-start = ((), (), s32[]{:S(2)}) async-start(), calls=%async_computation.3 | async-start | bytes 6782976 | tf_op jit(solution)/shard_map/all_gather | solution.py:86
  7.6 1.4 copy-start.3
  7.6 1.6 copy-start.4
  10.6 34.9 %copy-start.6 = (f32[1,2,360]{2,1,0:T(2,128)S(1)}, f32[1,2,360]{2,1,0:T(2,128)}, u32[]{:S(2)}) copy-start(f32[1,2,360]{2,1,0:T(2,128)} %param.17) | copy-start | bytes 8644
  45.5 99.8 %reduce-scatter.2.cloned.1.call-start = ((), (), s32[]{:S(2)}) async-start(), calls=%async_computation.4 | async-start | bytes 6782976 | tf_op jit(solution)/shard_map/reduce_scatter | solution.py:95
  84.6 6.0 %copy-start.7 = (bf16[1024,2880]{1,0:T(8,128)(2,1)S(1)}, bf16[1024,2880]{1,0:T(8,128)(2,1)}, u32[]{:S(2)}) copy-start(bf16[1024,2880]{1,0:T(8,128)(2,1)} %all-gather.2.cloned.1.call-done) | copy-start | bytes 17694724
  100.5 57.5 %copy-start.2 = (f32[32,2880]{1,0:T(8,128)S(1)}, f32[32,2880]{1,0:T(8,128)}, u32[]{:S(2)}) copy-start(f32[32,2880]{1,0:T(8,128)} %param.19) | copy-start | bytes 1105924
  147.7 30.7 %all-to-all-start.1 = ((bf16[32,4,2880]{2,1,0:T(4,128)(2,1)}), bf16[32,4,2880]{2,1,0:T(4,128)(2,1)S(1)}, u32[]{:S(2)}, u32[]{:S(2)}) async-start(bf16[32,4,2880]{2,1,0:T(4,128)(2,1)} %reshape.72), calls=%async_computation.2 | async-start | bytes 1507328 | tf_op jit(solution)/shard_map/all_to_all | solution.py:97
  158.1 1.7 copy-start.8
  158.1 2.9 %copy-start.5 = (s32[16,4]{0,1:T(4,128)S(1)}, s32[16,4]{0,1:T(4,128)}, u32[]{:S(2)}) copy-start(s32[16,4]{0,1:T(4,128)} %param.14) | copy-start | bytes 772
Sparse Core Ops, SparseCore 0:
  45.6 38.9 all-gather.1
  100.7 44.5 reduce-scatter.1
